TPU v7x, 128 devices: a whole 4x4x4 slice. The times are simulated.
128 devices in a mesh: azim: 16 (over y, z), plane: 8 (over x, core).
Axes of the slice: x: 4, y: 4, z: 4, core: 2. Of those that a mesh axis runs over, the one named last changes fastest.
Arguments:
- state: float32 [5, 192, 32768], P(None, 'azim', 'plane'), may hold values from -6 to 6
- speed: float32 [192, 32768], P('azim', 'plane'), may hold values from -2 to 2
- sigma: float32 [192, 32768], P('azim', 'plane'), may hold values from 1 to 24576
- dissipation: float32 [192, 32768], P('azim', 'plane'), may hold values from 0.05 to 1
- fringe: int32 [192, 32768], P('azim', 'plane'), may hold values from 0 to 1, as said below
- destination: int32 [2048, 1], P(('azim', 'plane')), may hold values from 0 to 7; in each aligned block of 16 rows (0 to 15, 16 to 31, ...) at most 4 rows name the same one
- donor: int32 [2048], P(('azim', 'plane')), may hold values from 0 to 11
- receptor: int32 [2048], P(('azim', 'plane')), may hold values from 0 to 11
- offset_y: int32 [2048], P(('azim', 'plane')), may hold values from 0 to 63
- offset_x: int32 [2048], P(('azim', 'plane')), may hold values from 0 to 63
- fraction_y: float32 [2048], P(('azim', 'plane')), may hold values from 0 to 1
- fraction_x: float32 [2048], P(('azim', 'plane')), may hold values from 0 to 1
Outputs:
- update: float32 [5, 192, 32768], P(None, 'azim', 'plane')
Inputs may be any that keep to these rules, and one draw needn't show every extreme that they name: The 16 entries of one device name each destination at most 4 times. `fringe`: a plane cell is a receptor at all of its 192 azimuthal rows or at none.
All inputs are finite; a program needn't handle non-finite values.
Results may differ from a plain program's by a relative error of at most 0.0003.
Values sent between devices are 32-bit elements; how exact they have to be, the bound alone decides.
A program may use at most 128 MiB of HBM per device.

v0:
```python
import functools

import jax
import jax.numpy as jnp
from jax import lax
from jax.experimental import pallas as pl
from jax.experimental.pallas import tpu as pltpu
from jax.sharding import PartitionSpec as P

TILE = 64
CAP = 4
FIELDS = 5
ROWS = 12
CELLS = TILE * TILE
LANES = 128
CHUNKS = CELLS // LANES
SLOTS = 16
COLS = FIELDS + 4
TIPS = 4 * COLS
BACK = 4 * FIELDS
MESH = pl.DeviceIdType.MESH
TIP_ROW = {0: 0, 1: 1, ROWS - 2: 2, ROWS - 1: 3}


def spread(source, dest, lead):
    def move(c, carry):
        lane = pl.multiple_of(c * LANES, LANES)
        row = pl.multiple_of(c * 8, 8)
        for f in range(lead):
            dest[f, 0, pl.ds(row, 8), :] = source[f, 0:8, pl.ds(lane, LANES)]
            dest[f, 1, pl.ds(row, 4), :] = source[f, 8:12, pl.ds(lane, LANES)]
        return carry

    lax.fori_loop(0, CHUNKS, move, 0, unroll=4)


def spread_flat(source, dest, slot):
    def move(c, carry):
        lane = pl.multiple_of(c * LANES, LANES)
        row = pl.multiple_of(c * 8, 8)
        dest[slot, 0, pl.ds(row, 8), :] = source[0:8, pl.ds(lane, LANES)]
        dest[slot, 1, pl.ds(row, 4), :] = source[8:12, pl.ds(lane, LANES)]
        return carry

    lax.fori_loop(0, CHUNKS, move, 0, unroll=4)


def prepare_kernel(
    destination,
    donor,
    receptor,
    offset_y,
    offset_x,
    fraction_y,
    fraction_x,
    state,
    speed,
    sigma,
    dissipation,
    packed,
    landing,
    tips,
    solved,
    cells,
    coefs,
    twice,
    counts,
):
    planes = landing.shape[0]
    spread(state, cells, FIELDS)
    for slot, source in enumerate((speed, sigma, dissipation)):
        spread_flat(source, coefs, slot)

    landing[...] = jnp.full(landing.shape, -1, jnp.int32)
    for d in range(planes):
        counts[d] = 0
    lane = lax.broadcasted_iota(jnp.int32, (CHUNKS, LANES), 1)
    column = lane & (TILE - 1)
    low_half = lane < TILE

    def one_entry(e, carry):
        target = destination[e, 0]
        rank = counts[target]
        counts[target] = rank + 1
        landing[target, pl.ds(rank, 1), :] = jnp.full((1, LANES), receptor[e], jnp.int32)
        row = donor[e]
        block = jnp.where(row >= 8, 1, 0)
        inner = row - 8 * block
        ox = offset_x[e]
        oy = offset_y[e]
        fx = fraction_x[e]
        fy = fraction_y[e]
        half = oy >> 1
        odd = (oy & 1) == 1
        even_first = jnp.where(odd, 0.0, 1.0 - fy)
        even_second = jnp.where(odd, fy, 0.0)
        odd_weight = jnp.where(odd, 1.0 - fy, fy)
        near = column + ox < TILE
        far = column + ox + 1 < TILE
        for f in range(FIELDS):
            tile = cells[f, block, pl.ds(inner, CHUNKS, stride=8), :]
            first = pltpu.roll(tile, LANES - ox, 1)
            second = pltpu.roll(tile, LANES - 1 - ox, 1)
            first = jnp.where(near, first, pltpu.roll(first, TILE, 1))
            second = jnp.where(far, second, pltpu.roll(second, TILE, 1))
            mixed = (1.0 - fx) * first + fx * second
            swapped = pltpu.roll(mixed, TILE, 1)
            twice[0, f, 0:CHUNKS, :] = mixed
            twice[0, f, CHUNKS : 2 * CHUNKS, :] = mixed
            twice[1, f, 0:CHUNKS, :] = swapped
            twice[1, f, CHUNKS : 2 * CHUNKS, :] = swapped
        for f in range(FIELDS):
            here = twice[0, f, pl.ds(half, CHUNKS), :]
            after = twice[0, f, pl.ds(half + 1, CHUNKS), :]
            odd_here = twice[1, f, pl.ds(half, CHUNKS), :]
            odd_after = twice[1, f, pl.ds(half + 1, CHUNKS), :]
            packed[target, rank, f] = (
                even_first * here
                + even_second * after
                + odd_weight * jnp.where(low_half, odd_here, odd_after)
            )
        return carry

    lax.fori_loop(0, SLOTS, one_entry, 0)

    def eliminate(part, carry):
        base = part * 64
        at = pl.ds(pl.multiple_of(part * 8, 8), 8)

        def load(ref, lead, r):
            return ref[lead, r // 8, pl.ds(base + r % 8, 8, stride=8), :]

        upper1 = []
        upper2 = []
        fields1 = fields2 = None
        for r in range(ROWS):
            c = load(coefs, 0, r)
            s = load(coefs, 1, r)
            d = load(coefs, 2, r)
            half = 0.5 * c
            common = -s - 4.0 * d
            a1 = common - half
            e1 = common + half
            centre = 1.0 + (2.0 * s + 10.0 * d)
            weight = 1.0 + 4.0 * d
            if r == 0:
                pivot, u1_top = centre, e1
            elif r == 1:
                pivot = centre - a1 * upper1[0]
                u1_top = e1 - a1 * upper2[0]
            else:
                spike_a1 = a1
                a1 = a1 - d * upper1[r - 2]
                pivot = centre - d * upper2[r - 2] - a1 * upper1[r - 1]
                u1_top = e1 - a1 * upper2[r - 1]
            inverse = 1.0 / pivot
            upper1.append(u1_top * inverse)
            upper2.append(d * inverse)
            now = []
            for k in range(FIELDS + 2):
                if k < FIELDS:
                    value = weight * load(cells, k, r)
                elif r == 0:
                    now.append((d if k == FIELDS else a1) * inverse)
                    continue
                elif r == 1 and k == FIELDS + 1:
                    value = d
                else:
                    value = None
                if r >= 1:
                    term = a1 * fields1[k]
                    value = -term if value is None else value - term
                if r >= 2:
                    value = value - d * fields2[k]
                now.append(value * inverse)
            for k in range(FIELDS + 2):
                solved[r, k, at, :] = now[k]
            fields2, fields1 = fields1, now

        later1 = later2 = None
        for r in range(ROWS - 1, -1, -1):
            now = []
            for k in range(COLS):
                if k < FIELDS + 2:
                    value = solved[r, k, at, :]
                elif r == ROWS - 1:
                    value = upper1[r] if k == FIELDS + 2 else upper2[r]
                elif r == ROWS - 2 and k == FIELDS + 2:
                    value = upper2[r]
                else:
                    value = None
                if r < ROWS - 1:
                    term = upper1[r] * later1[k]
                    value = -term if value is None else value - term
                if r < ROWS - 2:
                    value = value - upper2[r] * later2[k]
                now.append(value)
            for k in range(COLS):
                solved[r, k, at, :] = now[k]
            if r in TIP_ROW:
                for k in range(COLS):
                    tips[pl.ds(part * 8 * TIPS + TIP_ROW[r] * COLS + k, 8, stride=TIPS), :] = now[k]
            later2, later1 = later1, now
        return carry

    lax.fori_loop(0, CHUNKS // 8, eliminate, 0)


def merge(left, right):
    def pair(matrix, columns):
        return [matrix[i][0] * columns[0] + matrix[i][1] * columns[1] for i in range(2)]

    gs = slice(0, FIELDS)
    ws = slice(FIELDS, FIELDS + 2)
    vs = slice(FIELDS + 2, FIELDS + 4)
    left_v = [[left[i][FIELDS + 2 + m] for m in range(2)] for i in range(4)]
    right_w = [[right[i][FIELDS + m] for m in range(2)] for i in range(4)]
    nothing = jnp.zeros((2,) + left[0].shape[1:], jnp.float32)
    product = [
        [sum(right_w[i][m] * left_v[2 + m][j] for m in range(2)) for j in range(2)]
        for i in range(2)
    ]
    m00, m01 = 1.0 - product[0][0], -product[0][1]
    m10, m11 = -product[1][0], 1.0 - product[1][1]
    scale = 1.0 / (m00 * m11 - m01 * m10)
    inverse = [[m11 * scale, -m01 * scale], [-m10 * scale, m00 * scale]]
    known = [jnp.concatenate([left[2 + i][gs], left[2 + i][ws]], axis=0) for i in range(2)]
    through = pair(right_w[:2], known)
    raw = [
        jnp.concatenate(
            [right[i][gs] - through[i][gs], -through[i][FIELDS:], right[i][vs]], axis=0
        )
        for i in range(2)
    ]
    inner_a = pair(inverse, raw)
    from_a = pair(left_v[2:], inner_a)
    inner_b = [
        jnp.concatenate([left[2 + i][gs], left[2 + i][ws], nothing], axis=0) - from_a[i]
        for i in range(2)
    ]
    from_a = pair(left_v[:2], inner_a)
    outer_a = [
        jnp.concatenate([left[i][gs], left[i][ws], nothing], axis=0) - from_a[i] for i in range(2)
    ]
    from_b = pair(right_w[2:], inner_b)
    outer_b = [
        jnp.concatenate([right[2 + i][gs], nothing, right[2 + i][vs]], axis=0) - from_b[i]
        for i in range(2)
    ]
    return outer_a + outer_b


def close(block):
    matrix = []
    for i in range(4):
        line = [block[i][FIELDS + 2], block[i][FIELDS + 3], block[i][FIELDS], block[i][FIELDS + 1]]
        line[i] = 1.0 + line[i]
        matrix.append(line)
    values = [block[i][0:FIELDS] for i in range(4)]
    for p in range(4):
        scale = 1.0 / matrix[p][p]
        for c in range(p + 1, 4):
            matrix[p][c] = matrix[p][c] * scale
        values[p] = values[p] * scale
        for r in range(p + 1, 4):
            for c in range(p + 1, 4):
                matrix[r][c] = matrix[r][c] - matrix[r][p] * matrix[p][c]
            values[r] = values[r] - matrix[r][p] * values[p]
    for r in range(2, -1, -1):
        for c in range(r + 1, 4):
            values[r] = values[r] - matrix[r][c] * values[c]
    return values


def exchange_kernel(
    azims,
    planes,
    packed,
    landing,
    tips,
    packed_in,
    landing_in,
    borders,
    tips_in,
    ping,
    pong,
    firsts,
    answers,
    tile_send,
    tile_recv,
    land_send,
    land_recv,
    tips_send,
    tips_recv,
    back_send,
    back_recv,
    own_sem,
):
    a = lax.axis_index("azim")
    p = lax.axis_index("plane")
    per = CHUNKS // azims
    tip_rows = per * TIPS
    back_rows = per * BACK

    barrier = pltpu.get_barrier_semaphore()
    for o in range(1, planes):
        pl.semaphore_signal(
            barrier, inc=1, device_id=(a, lax.rem(p + o, planes)), device_id_type=MESH
        )
    for o in range(1, azims):
        pl.semaphore_signal(
            barrier, inc=1, device_id=(lax.rem(a + o, azims), p), device_id_type=MESH
        )
    pl.semaphore_wait(barrier, planes + azims - 2)

    def to_azim(source, dest, rows, send, recv, o):
        there = lax.rem(a + o, azims)
        return pltpu.make_async_remote_copy(
            src_ref=source.at[pl.ds(pl.multiple_of(there * rows, 8), rows), :],
            dst_ref=dest.at[pl.ds(pl.multiple_of(a * rows, 8), rows), :],
            send_sem=send.at[o],
            recv_sem=recv.at[o],
            device_id=(there, p),
            device_id_type=MESH,
        )

    def own_azim(source, dest, rows, index):
        at = pl.ds(pl.multiple_of(a * rows, 8), rows)
        return pltpu.make_async_copy(source.at[at, :], dest.at[at, :], own_sem.at[index])

    def to_plane(o):
        there = lax.rem(p + o, planes)
        return (
            pltpu.make_async_remote_copy(
                src_ref=packed.at[there],
                dst_ref=packed_in.at[p],
                send_sem=tile_send.at[o],
                recv_sem=tile_recv.at[o],
                device_id=(a, there),
                device_id_type=MESH,
            ),
            pltpu.make_async_remote_copy(
                src_ref=landing.at[there],
                dst_ref=landing_in.at[p],
                send_sem=land_send.at[o],
                recv_sem=land_recv.at[o],
                device_id=(a, there),
                device_id_type=MESH,
            ),
        )

    tip_copies = [to_azim(tips, tips_in, tip_rows, tips_send, tips_recv, o) for o in range(1, azims)]
    for copy in tip_copies:
        copy.start()
    own_tips = own_azim(tips, tips_in, tip_rows, 0)
    own_tips.start()
    tile_copies = []
    for o in range(1, planes):
        tile_copies.extend(to_plane(o))
    for copy in tile_copies:
        copy.start()
    own_tiles = pltpu.make_async_copy(packed.at[p], packed_in.at[p], own_sem.at[2])
    own_land = pltpu.make_async_copy(landing.at[p], landing_in.at[p], own_sem.at[3])
    own_tiles.start()
    own_land.start()

    own_tips.wait()
    for copy in tip_copies:
        copy.wait()

    for v in range(TIPS):
        value = tips_in[pl.ds(v, CHUNKS, stride=TIPS), :]
        ping[v, 0:CHUNKS, :] = value
        ping[v, CHUNKS : 2 * CHUNKS, :] = value

    source, dest = ping, pong
    step = 1
    while step < azims:

        def level(part, carry, source=source, dest=dest, shift=step * per):
            row = pl.multiple_of(part * 8, 8)
            left = [source[COLS * i : COLS * (i + 1), pl.ds(row, 8), :] for i in range(4)]
            right = [source[COLS * i : COLS * (i + 1), pl.ds(row + shift, 8), :] for i in range(4)]
            for i, value in enumerate(merge(left, right)):
                dest[COLS * i : COLS * (i + 1), pl.ds(row, 8), :] = value
                dest[COLS * i : COLS * (i + 1), pl.ds(row + CHUNKS, 8), :] = value
            return carry

        lax.fori_loop(0, CHUNKS // 8, level, 0)
        source, dest = dest, source
        step *= 2

    def last(part, carry):
        row = pl.multiple_of(part * 8, 8)
        block = [source[COLS * i : COLS * (i + 1), pl.ds(row, 8), :] for i in range(4)]
        values = close(block)
        for i in range(2):
            firsts[FIELDS * i : FIELDS * (i + 1), pl.ds(row, 8), :] = values[i]
            firsts[FIELDS * i : FIELDS * (i + 1), pl.ds(row + CHUNKS, 8), :] = values[i]
            for f in range(FIELDS):
                answers[pl.ds(part * 8 * BACK + i * FIELDS + f, 8, stride=BACK), :] = values[2 + i][f]
        return carry

    lax.fori_loop(0, CHUNKS // 8, last, 0)
    for v in range(2 * FIELDS):
        answers[pl.ds(2 * FIELDS + v, CHUNKS, stride=BACK), :] = firsts[v, per : per + CHUNKS, :]

    back_copies = [
        to_azim(answers, borders, back_rows, back_send, back_recv, o) for o in range(1, azims)
    ]
    for copy in back_copies:
        copy.start()
    own_back = own_azim(answers, borders, back_rows, 1)
    own_back.start()
    own_back.wait()
    for copy in back_copies:
        copy.wait()
    own_tiles.wait()
    own_land.wait()
    for copy in tile_copies:
        copy.wait()


def finish_kernel(landing, packed, borders, solved, state, fringe, out, cells, mask, total, counts):
    planes = landing.shape[0]
    spread(state, cells, FIELDS)
    for c in range(CHUNKS):
        mask[c : c + 1, :] = fringe[0:1, c * LANES : (c + 1) * LANES]
    for r in range(ROWS):
        counts[r] = 0.0
    total[...] = jnp.zeros(total.shape, jnp.float32)

    def add(slot, carry):
        d = slot // CAP
        k = slot - d * CAP
        row = landing[d, k, 0]

        @pl.when(row >= 0)
        def _():
            total[row] = total[row] + packed[d, k]
            counts[row] = counts[row] + 1.0

        return carry

    lax.fori_loop(0, planes * CAP, add, 0)

    def part_of(part, carry):
        at = pl.ds(pl.multiple_of(part * 8, 8), 8)
        chosen = mask[at, :] == 1
        previous = [
            [
                borders[pl.ds(part * 8 * BACK + i * FIELDS + f, 8, stride=BACK), :]
                for f in range(FIELDS)
            ]
            for i in range(2)
        ]
        following = [
            [
                borders[pl.ds(part * 8 * BACK + (2 + i) * FIELDS + f, 8, stride=BACK), :]
                for f in range(FIELDS)
            ]
            for i in range(2)
        ]
        for r in range(ROWS):
            w = [solved[r, FIELDS + i, at, :] for i in range(2)]
            v = [solved[r, FIELDS + 2 + i, at, :] for i in range(2)]
            count = counts[r]
            for f in range(FIELDS):
                where = (f, r // 8, pl.ds(part * 64 + r % 8, 8, stride=8))
                q = cells[where + (slice(None),)]
                value = solved[r, f, at, :] - q
                for i in range(2):
                    value = value - w[i] * previous[i][f] - v[i] * following[i][f]
                relaxed = (total[r, f, at, :] - count * q) / (count + 1.0)
                cells[where + (slice(None),)] = jnp.where(chosen, relaxed, value)
        return carry

    lax.fori_loop(0, CHUNKS // 8, part_of, 0)

    def move(c, carry):
        lane = pl.multiple_of(c * LANES, LANES)
        row = pl.multiple_of(c * 8, 8)
        for f in range(FIELDS):
            out[f, 0:8, pl.ds(lane, LANES)] = cells[f, 0, pl.ds(row, 8), :]
            out[f, 8:12, pl.ds(lane, LANES)] = cells[f, 1, pl.ds(row, 4), :]
        return carry

    lax.fori_loop(0, CHUNKS, move, 0, unroll=4)


def f32(*shape):
    return jax.ShapeDtypeStruct(shape, jnp.float32)


def local(
    state,
    speed,
    sigma,
    dissipation,
    fringe,
    destination,
    donor,
    receptor,
    offset_y,
    offset_x,
    fraction_y,
    fraction_x,
):
    azims = lax.axis_size("azim")
    planes = lax.axis_size("plane")
    vmem = pl.BlockSpec(memory_space=pltpu.VMEM)
    smem = pl.BlockSpec(memory_space=pltpu.SMEM)
    anywhere = pl.BlockSpec(memory_space=pl.ANY)
    packed, landing, tips, solved = pl.pallas_call(
        prepare_kernel,
        out_shape=(
            f32(planes, CAP, FIELDS, CHUNKS, LANES),
            jax.ShapeDtypeStruct((planes, 8, LANES), jnp.int32),
            f32(CHUNKS * TIPS, LANES),
            f32(ROWS, COLS, CHUNKS, LANES),
        ),
        in_specs=[smem] * 7 + [vmem] * 4,
        out_specs=(vmem,) * 4,
        scratch_shapes=[
            pltpu.VMEM((FIELDS, 2, CHUNKS * 8, LANES), jnp.float32),
            pltpu.VMEM((3, 2, CHUNKS * 8, LANES), jnp.float32),
            pltpu.VMEM((2, FIELDS, 2 * CHUNKS, LANES), jnp.float32),
            pltpu.SMEM((planes,), jnp.int32),
        ],
        compiler_params=pltpu.CompilerParams(vmem_limit_bytes=32 * 2**20),
        name="prepare",
    )(
        destination,
        donor,
        receptor,
        offset_y,
        offset_x,
        fraction_y,
        fraction_x,
        state,
        speed,
        sigma,
        dissipation,
    )
    packed_in, landing_in, borders = pl.pallas_call(
        functools.partial(exchange_kernel, azims, planes),
        out_shape=(
            f32(planes, CAP, FIELDS, CHUNKS, LANES),
            jax.ShapeDtypeStruct((planes, 8, LANES), jnp.int32),
            f32(CHUNKS * BACK, LANES),
        ),
        in_specs=[anywhere, anywhere, vmem],
        out_specs=(anywhere, anywhere, vmem),
        scratch_shapes=[
            pltpu.VMEM((CHUNKS * TIPS, LANES), jnp.float32),
            pltpu.VMEM((TIPS, 2 * CHUNKS, LANES), jnp.float32),
            pltpu.VMEM((TIPS, 2 * CHUNKS, LANES), jnp.float32),
            pltpu.VMEM((2 * FIELDS, 2 * CHUNKS, LANES), jnp.float32),
            pltpu.VMEM((CHUNKS * BACK, LANES), jnp.float32),
            pltpu.SemaphoreType.DMA((planes,)),
            pltpu.SemaphoreType.DMA((planes,)),
            pltpu.SemaphoreType.DMA((planes,)),
            pltpu.SemaphoreType.DMA((planes,)),
            pltpu.SemaphoreType.DMA((azims,)),
            pltpu.SemaphoreType.DMA((azims,)),
            pltpu.SemaphoreType.DMA((azims,)),
            pltpu.SemaphoreType.DMA((azims,)),
            pltpu.SemaphoreType.DMA((4,)),
        ],
        compiler_params=pltpu.CompilerParams(
            collective_id=0, has_side_effects=True, vmem_limit_bytes=32 * 2**20
        ),
        name="exchange",
    )(packed, landing, tips)
    return pl.pallas_call(
        finish_kernel,
        out_shape=f32(FIELDS, ROWS, CELLS),
        in_specs=[smem] + [vmem] * 5,
        out_specs=vmem,
        scratch_shapes=[
            pltpu.VMEM((FIELDS, 2, CHUNKS * 8, LANES), jnp.float32),
            pltpu.VMEM((CHUNKS, LANES), jnp.int32),
            pltpu.VMEM((ROWS, FIELDS, CHUNKS, LANES), jnp.float32),
            pltpu.SMEM((ROWS,), jnp.float32),
        ],
        compiler_params=pltpu.CompilerParams(vmem_limit_bytes=32 * 2**20),
        name="finish",
    )(landing_in, packed_in, borders, solved, state, fringe)


def solution(mesh):
    in_specs = (
        P(None, "azim", "plane"),
        P("azim", "plane"),
        P("azim", "plane"),
        P("azim", "plane"),
        P("azim", "plane"),
        P(("azim", "plane"), None),
        P(("azim", "plane")),
        P(("azim", "plane")),
        P(("azim", "plane")),
        P(("azim", "plane")),
        P(("azim", "plane")),
        P(("azim", "plane")),
    )
    out_specs = P(None, "azim", "plane")
    return jax.shard_map(local, mesh=mesh, in_specs=in_specs, out_specs=out_specs, check_vma=False)
```

profile of v0, /device:TPU:1, one launch (start us, length us, event | category | flops | bytes accessed | tf_op | source)
XLA Modules:
  0.0 59.7 jit_solution(15348470968489355830)
XLA Ops:
  0.0 0.7 %copy.13.destination = s32[16,1]{1,0:T(8,128)S(1)} copy(s32[16,1]{0,1:T(1,128)} %param.17) | data formatting | bytes 128 | tf_op args[5]
  0.7 0.0 copy-start
  0.7 1.3 %copy-done = f32[5,12,4096]{2,1,0:T(8,128)S(1)} copy-done((f32[5,12,4096]{2,1,0:T(8,128)S(1)}, f32[5,12,4096]{2,1,0:T(8,128)}, u32[]{:S(2)}) %copy-start) | copy-done | bytes 983064
  2.0 0.0 copy-start.2
  2.1 0.9 %copy-done.2 = f32[12,4096]{1,0:T(8,128)S(1)} copy-done((f32[12,4096]{1,0:T(8,128)S(1)}, f32[12,4096]{1,0:T(8,128)}, u32[]{:S(2)}) %copy-start.2) | copy-done | bytes 196632
  3.0 0.0 copy-start.3
  3.0 0.9 %copy-done.3 = f32[12,4096]{1,0:T(8,128)S(1)} copy-done((f32[12,4096]{1,0:T(8,128)S(1)}, f32[12,4096]{1,0:T(8,128)}, u32[]{:S(2)}) %copy-start.3) | copy-done | bytes 196632
  4.0 0.0 copy-start.4
  4.0 0.9 %copy-done.4 = f32[12,4096]{1,0:T(8,128)S(1)} copy-done((f32[12,4096]{1,0:T(8,128)S(1)}, f32[12,4096]{1,0:T(8,128)}, u32[]{:S(2)}) %copy-start.4) | copy-done | bytes 196632
  4.9 0.0 copy-start.6
  4.9 0.7 %copy-done.6 = s32[16]{0:T(128)S(1)} copy-done((s32[16]{0:T(128)S(1)}, s32[16]{0:T(128)}, u32[]{:S(2)}) %copy-start.6) | copy-done | bytes 88
  5.6 0.0 copy-start.7
  5.6 0.7 %copy-done.7 = s32[16]{0:T(128)S(1)} copy-done((s32[16]{0:T(128)S(1)}, s32[16]{0:T(128)}, u32[]{:S(2)}) %copy-start.7) | copy-done | bytes 88
  6.2 0.0 copy-start.8
  6.2 0.7 %copy-done.8 = s32[16]{0:T(128)S(1)} copy-done((s32[16]{0:T(128)S(1)}, s32[16]{0:T(128)}, u32[]{:S(2)}) %copy-start.8) | copy-done | bytes 88
  6.9 0.0 copy-start.9
  6.9 0.7 %copy-done.9 = s32[16]{0:T(128)S(1)} copy-done((s32[16]{0:T(128)S(1)}, s32[16]{0:T(128)}, u32[]{:S(2)}) %copy-start.9) | copy-done | bytes 88
  7.5 0.0 copy-start.10
  7.5 0.7 %copy-done.10 = f32[16]{0:T(128)S(1)} copy-done((f32[16]{0:T(128)S(1)}, f32[16]{0:T(128)}, u32[]{:S(2)}) %copy-start.10) | copy-done | bytes 88
  8.2 0.0 copy-start.11
  8.2 0.7 %copy-done.11 = f32[16]{0:T(128)S(1)} copy-done((f32[16]{0:T(128)S(1)}, f32[16]{0:T(128)}, u32[]{:S(2)}) %copy-start.11) | copy-done | bytes 88
  8.8 6.3 %prepare.1 = (f32[8,4,5,32,128]{4,3,2,1,0:T(8,128)S(1)}, s32[8,8,128]{2,1,0:T(8,128)S(1)}, f32[1152,128]{1,0:T(8,128)S(1)}, f32[12,9,32,128]{3,2,1,0:T(8,128)S(1)}) custom-call(s32[16,1]{1,0:T(8,128)S(1)} %copy.13.destination, s32[16]{0:T(128)S(1)} %copy-done.6, s32[16]{0:T(128)S(1)} %copy-done.7, s32[16]{0:T(128)S(1)} %copy-done.8, s32[16]{0:T(128)S(1)} %copy-done.9, ...), custom_call_target="tpu_custom_call" | custom-call | tf_op jit(solution)/shard_map/prepare/pallas_call | solution.py:514
  15.1 0.0 copy-start.1
  15.1 0.0 copy-start.5
  15.1 40.5 %exchange.1 = (f32[8,4,5,32,128]{4,3,2,1,0:T(8,128)S(1)}, s32[8,8,128]{2,1,0:T(8,128)S(1)}, f32[640,128]{1,0:T(8,128)S(1)}) custom-call(f32[8,4,5,32,128]{4,3,2,1,0:T(8,128)S(1)} %get-tuple-element.12.packed, s32[8,8,128]{2,1,0:T(8,128)S(1)} %get-tuple-element.13.landing, f32[1152,128]{1,0:T(8,128)S(1)} %get-tuple-element.14.tips), custom_call_target="tpu_custom_call" | custom-call | tf_op jit(solution)/shard_map/exchange/pallas_call | solution.py:545
  55.7 0.0 copy-done.1
  55.7 0.0 copy-done.5
  55.7 4.0 %finish.1 = f32[5,12,4096]{2,1,0:T(8,128)} custom-call(s32[8,8,128]{2,1,0:T(8,128)S(1)} %get-tuple-element.15.landing, f32[8,4,5,32,128]{4,3,2,1,0:T(8,128)S(1)} %get-tuple-element.16.packed, f32[640,128]{1,0:T(8,128)S(1)} %get-tuple-element.17.borders, f32[12,9,32,128]{3,2,1,0:T(8,128)S(1)} %get-tuple-element.18.solved, f32[5,12,4096]{2,1,0:T(8,128)S(1)} %copy-done.1, ...), custom_call_target="tpu_custom_call" | custom-call | tf_op jit(solution)/shard_map/finish/pallas_call | solution.py:575
Async XLA Ops:
  0.7 1.3 %copy-start = (f32[5,12,4096]{2,1,0:T(8,128)S(1)}, f32[5,12,4096]{2,1,0:T(8,128)}, u32[]{:S(2)}) copy-start(f32[5,12,4096]{2,1,0:T(8,128)} %state.3) | copy-start | bytes 2949124
  2.0 0.9 %copy-start.2 = (f32[12,4096]{1,0:T(8,128)S(1)}, f32[12,4096]{1,0:T(8,128)}, u32[]{:S(2)}) copy-start(f32[12,4096]{1,0:T(8,128)} %speed.1) | copy-start | bytes 589828
  3.0 0.9 %copy-start.3 = (f32[12,4096]{1,0:T(8,128)S(1)}, f32[12,4096]{1,0:T(8,128)}, u32[]{:S(2)}) copy-start(f32[12,4096]{1,0:T(8,128)} %sigma.1) | copy-start | bytes 589828
  4.0 0.9 %copy-start.4 = (f32[12,4096]{1,0:T(8,128)S(1)}, f32[12,4096]{1,0:T(8,128)}, u32[]{:S(2)}) copy-start(f32[12,4096]{1,0:T(8,128)} %dissipation.1) | copy-start | bytes 589828
  4.9 0.7 %copy-start.6 = (s32[16]{0:T(128)S(1)}, s32[16]{0:T(128)}, u32[]{:S(2)}) copy-start(s32[16]{0:T(128)} %donor.1) | copy-start | bytes 196
  5.6 0.7 %copy-start.7 = (s32[16]{0:T(128)S(1)}, s32[16]{0:T(128)}, u32[]{:S(2)}) copy-start(s32[16]{0:T(128)} %receptor.1) | copy-start | bytes 196
  6.2 0.7 %copy-start.8 = (s32[16]{0:T(128)S(1)}, s32[16]{0:T(128)}, u32[]{:S(2)}) copy-start(s32[16]{0:T(128)} %offset_y.1) | copy-start | bytes 196
  6.9 0.7 %copy-start.9 = (s32[16]{0:T(128)S(1)}, s32[16]{0:T(128)}, u32[]{:S(2)}) copy-start(s32[16]{0:T(128)} %offset_x.1) | copy-start | bytes 196
  7.5 0.7 %copy-start.10 = (f32[16]{0:T(128)S(1)}, f32[16]{0:T(128)}, u32[]{:S(2)}) copy-start(f32[16]{0:T(128)} %fraction_y.1) | copy-start | bytes 196
  8.2 0.7 %copy-start.11 = (f32[16]{0:T(128)S(1)}, f32[16]{0:T(128)}, u32[]{:S(2)}) copy-start(f32[16]{0:T(128)} %fraction_x.1) | copy-start | bytes 196
  15.1 40.6 %copy-start.1 = (f32[5,12,4096]{2,1,0:T(8,128)S(1)}, f32[5,12,4096]{2,1,0:T(8,128)}, u32[]{:S(2)}) copy-start(f32[5,12,4096]{2,1,0:T(8,128)} %state.3) | copy-start | bytes 2949124
  15.1 40.5 %copy-start.5 = (s32[12,4096]{1,0:T(8,128)S(1)}, s32[12,4096]{1,0:T(8,128)}, u32[]{:S(2)}) copy-start(s32[12,4096]{1,0:T(8,128)} %fringe.1) | copy-start | bytes 589828
where the time goes:
time: 59.9 us; the launch traced here: 59.7 us
  Pallas kernels  50.8 us (85%)
  local copies, waits for them, and re-layouts  8.84 us (15%)
    pallas_call x1, Pallas kernels, local(): pl.pallas_call(functools.partial(exchange_kernel, azims, planes), out_sha...  40.5 us
    unnamed x25, local copies, waits for them, and re-layouts  8.84 us
    pallas_call x1, Pallas kernels, local(): pl.pallas_call(prepare_kernel, out_shape=(f32(planes, CAP, FIELDS, CHUNKS...  6.27 us
    pallas_call x1, Pallas kernels, local(): pl.pallas_call(finish_kernel, out_shape=f32(FIELDS, ROWS, CELLS), in_spec...  3.97 us

commit v1 on v0

v1 whole, which is shorter than its diff:
```python
import functools

import jax
import jax.numpy as jnp
from jax import lax
from jax.experimental import pallas as pl
from jax.experimental.pallas import tpu as pltpu
from jax.sharding import PartitionSpec as P

TILE = 64
CAP = 4
FIELDS = 5
ROWS = 12
CELLS = TILE * TILE
LANES = 128
CHUNKS = CELLS // LANES
SLOTS = 16
COLS = FIELDS + 4
TIPS = 4 * COLS
BACK = 4 * FIELDS
MESH = pl.DeviceIdType.MESH
TIP_ROW = {0: 0, 1: 1, ROWS - 2: 2, ROWS - 1: 3}


def spread(source, dest):
    def move(c, carry):
        lane = pl.multiple_of(c * LANES, LANES)
        row = pl.multiple_of(c * 8, 8)
        for f in range(source.shape[0]):
            dest[f, 0, pl.ds(row, 8), :] = source[f, 0:8, pl.ds(lane, LANES)]
            dest[f, 1, pl.ds(row, 4), :] = source[f, 8:12, pl.ds(lane, LANES)]
        return carry

    lax.fori_loop(0, CHUNKS, move, 0, unroll=4)


def eliminate(cells, coefs, solved, tips, part):
    base = part * 64
    at = pl.ds(pl.multiple_of(part * 8, 8), 8)

    def load(ref, lead, r):
        return ref[lead, r // 8, pl.ds(base + r % 8, 8, stride=8), :]

    upper1 = []
    upper2 = []
    fields1 = fields2 = None
    for r in range(ROWS):
        c = load(coefs, 0, r)
        s = load(coefs, 1, r)
        d = load(coefs, 2, r)
        half = 0.5 * c
        common = -s - 4.0 * d
        a1 = common - half
        e1 = common + half
        centre = 1.0 + (2.0 * s + 10.0 * d)
        weight = 1.0 + 4.0 * d
        if r == 0:
            pivot, u1_top = centre, e1
        elif r == 1:
            pivot = centre - a1 * upper1[0]
            u1_top = e1 - a1 * upper2[0]
        else:
            a1 = a1 - d * upper1[r - 2]
            pivot = centre - d * upper2[r - 2] - a1 * upper1[r - 1]
            u1_top = e1 - a1 * upper2[r - 1]
        inverse = 1.0 / pivot
        upper1.append(u1_top * inverse)
        upper2.append(d * inverse)
        now = []
        for k in range(FIELDS + 2):
            if k < FIELDS:
                value = weight * load(cells, k, r)
            elif r == 0:
                now.append((d if k == FIELDS else a1) * inverse)
                continue
            elif r == 1 and k == FIELDS + 1:
                value = d
            else:
                value = None
            if r >= 1:
                term = a1 * fields1[k]
                value = -term if value is None else value - term
            if r >= 2:
                value = value - d * fields2[k]
            now.append(value * inverse)
        for k in range(FIELDS + 2):
            solved[r, k, at, :] = now[k]
        fields2, fields1 = fields1, now

    later1 = later2 = None
    for r in range(ROWS - 1, -1, -1):
        now = []
        for k in range(COLS):
            if k < FIELDS + 2:
                value = solved[r, k, at, :]
            elif r == ROWS - 1:
                value = upper1[r] if k == FIELDS + 2 else upper2[r]
            elif r == ROWS - 2 and k == FIELDS + 2:
                value = upper2[r]
            else:
                value = None
            if r < ROWS - 1:
                term = upper1[r] * later1[k]
                value = -term if value is None else value - term
            if r < ROWS - 2:
                value = value - upper2[r] * later2[k]
            now.append(value)
        for k in range(COLS):
            solved[r, k, at, :] = now[k]
        if r in TIP_ROW:
            for k in range(COLS):
                tips[pl.ds(part * 8 * TIPS + TIP_ROW[r] * COLS + k, 8, stride=TIPS), :] = now[k]
        later2, later1 = later1, now


def merge(left, right):
    def pair(matrix, columns):
        return [matrix[i][0] * columns[0] + matrix[i][1] * columns[1] for i in range(2)]

    gs = slice(0, FIELDS)
    ws = slice(FIELDS, FIELDS + 2)
    vs = slice(FIELDS + 2, FIELDS + 4)
    left_v = [[left[i][FIELDS + 2 + m] for m in range(2)] for i in range(4)]
    right_w = [[right[i][FIELDS + m] for m in range(2)] for i in range(4)]
    nothing = jnp.zeros((2,) + left[0].shape[1:], jnp.float32)
    product = [
        [sum(right_w[i][m] * left_v[2 + m][j] for m in range(2)) for j in range(2)]
        for i in range(2)
    ]
    m00, m01 = 1.0 - product[0][0], -product[0][1]
    m10, m11 = -product[1][0], 1.0 - product[1][1]
    scale = 1.0 / (m00 * m11 - m01 * m10)
    inverse = [[m11 * scale, -m01 * scale], [-m10 * scale, m00 * scale]]
    known = [jnp.concatenate([left[2 + i][gs], left[2 + i][ws]], axis=0) for i in range(2)]
    through = pair(right_w[:2], known)
    raw = [
        jnp.concatenate(
            [right[i][gs] - through[i][gs], -through[i][FIELDS:], right[i][vs]], axis=0
        )
        for i in range(2)
    ]
    inner_a = pair(inverse, raw)
    from_a = pair(left_v[2:], inner_a)
    inner_b = [
        jnp.concatenate([left[2 + i][gs], left[2 + i][ws], nothing], axis=0) - from_a[i]
        for i in range(2)
    ]
    from_a = pair(left_v[:2], inner_a)
    outer_a = [
        jnp.concatenate([left[i][gs], left[i][ws], nothing], axis=0) - from_a[i] for i in range(2)
    ]
    from_b = pair(right_w[2:], inner_b)
    outer_b = [
        jnp.concatenate([right[2 + i][gs], nothing, right[2 + i][vs]], axis=0) - from_b[i]
        for i in range(2)
    ]
    return outer_a + outer_b


def close(block):
    matrix = []
    for i in range(4):
        line = [block[i][FIELDS + 2], block[i][FIELDS + 3], block[i][FIELDS], block[i][FIELDS + 1]]
        line[i] = 1.0 + line[i]
        matrix.append(line)
    values = [block[i][0:FIELDS] for i in range(4)]
    for p in range(4):
        scale = 1.0 / matrix[p][p]
        for c in range(p + 1, 4):
            matrix[p][c] = matrix[p][c] * scale
        values[p] = values[p] * scale
        for r in range(p + 1, 4):
            for c in range(p + 1, 4):
                matrix[r][c] = matrix[r][c] - matrix[r][p] * matrix[p][c]
            values[r] = values[r] - matrix[r][p] * values[p]
    for r in range(2, -1, -1):
        for c in range(r + 1, 4):
            values[r] = values[r] - matrix[r][c] * values[c]
    return values


def exchange_kernel(
    azims,
    planes,
    destination_hbm,
    donor_hbm,
    receptor_hbm,
    offset_y_hbm,
    offset_x_hbm,
    fraction_y_hbm,
    fraction_x_hbm,
    state_hbm,
    speed_hbm,
    sigma_hbm,
    dissipation_hbm,
    packed_in,
    landing_in,
    update,
    destination,
    donor,
    receptor,
    offset_y,
    offset_x,
    fraction_y,
    fraction_x,
    entries,
    state,
    raw_coefs,
    cells,
    coefs,
    twice,
    packed,
    landing,
    solved,
    tips,
    tips_in,
    ping,
    pong,
    firsts,
    answers,
    borders,
    small_sem,
    large_sem,
    tile_send,
    tile_recv,
    land_send,
    land_recv,
    tips_send,
    tips_recv,
    back_send,
    back_recv,
    own_sem,
):
    a = lax.axis_index("azim")
    p = lax.axis_index("plane")
    per = CHUNKS // azims
    tip_rows = per * TIPS
    back_rows = per * BACK
    chips = planes // 2

    small = [
        pltpu.make_async_copy(source, dest, small_sem.at[i])
        for i, (source, dest) in enumerate(
            (
                (destination_hbm, destination),
                (donor_hbm, donor),
                (receptor_hbm, receptor),
                (offset_y_hbm, offset_y),
                (offset_x_hbm, offset_x),
                (fraction_y_hbm, fraction_y),
                (fraction_x_hbm, fraction_x),
            )
        )
    ]
    large = [
        pltpu.make_async_copy(source, dest, large_sem.at[i])
        for i, (source, dest) in enumerate(
            (
                (state_hbm, state),
                (speed_hbm, raw_coefs.at[0]),
                (sigma_hbm, raw_coefs.at[1]),
                (dissipation_hbm, raw_coefs.at[2]),
            )
        )
    ]
    for copy in small:
        copy.start()
    for copy in large:
        copy.start()

    barrier = pltpu.get_barrier_semaphore()
    for o in range(1, planes):
        pl.semaphore_signal(
            barrier, inc=1, device_id=(a, lax.rem(p + o, planes)), device_id_type=MESH
        )
    for o in range(1, azims):
        pl.semaphore_signal(
            barrier, inc=1, device_id=(lax.rem(a + o, azims), p), device_id_type=MESH
        )

    def to_azim(source, dest, rows, send, recv, o):
        there = lax.rem(a + o, azims)
        return pltpu.make_async_remote_copy(
            src_ref=source.at[pl.ds(pl.multiple_of(there * rows, 8), rows), :],
            dst_ref=dest.at[pl.ds(pl.multiple_of(a * rows, 8), rows), :],
            send_sem=send.at[o],
            recv_sem=recv.at[o],
            device_id=(there, p),
            device_id_type=MESH,
        )

    def own_azim(source, dest, rows, index):
        at = pl.ds(pl.multiple_of(a * rows, 8), rows)
        return pltpu.make_async_copy(source.at[at, :], dest.at[at, :], own_sem.at[index])

    def plane_peer(i):
        chip = lax.rem(p // 2 + chips - 1 - lax.rem(i, chips), chips)
        core = lax.rem(p + 1 - i // chips, 2)
        return chip * 2 + core

    def to_plane(i):
        there = plane_peer(i)
        return (
            pltpu.make_async_remote_copy(
                src_ref=packed.at[i],
                dst_ref=packed_in.at[p],
                send_sem=tile_send.at[i],
                recv_sem=tile_recv.at[i],
                device_id=(a, there),
                device_id_type=MESH,
            ),
            pltpu.make_async_remote_copy(
                src_ref=landing.at[i],
                dst_ref=landing_in.at[p],
                send_sem=land_send.at[i],
                recv_sem=land_recv.at[i],
                device_id=(a, there),
                device_id_type=MESH,
            ),
        )

    lane = lax.broadcasted_iota(jnp.int32, (CHUNKS, LANES), 1)
    column = lane & (TILE - 1)
    low_half = lane < TILE

    for copy in small:
        copy.wait()
    large[0].wait()
    spread(state, cells)
    pl.semaphore_wait(barrier, planes + azims - 2)

    def fill(i, carry):
        target = plane_peer(i)
        seen = jnp.int32(0)
        found = [jnp.int32(-1)] * CAP
        for e in range(SLOTS):
            match = destination[e] == target
            for k in range(CAP):
                found[k] = jnp.where(match & (seen == k), e, found[k])
            seen = seen + jnp.where(match, 1, 0)
        for k in range(CAP):
            entries[k] = found[k]

        def one_slot(k, inner_carry):
            entry = entries[k]
            e = jnp.maximum(entry, 0)
            place = jnp.where(entry >= 0, receptor[e], -1)
            landing[i, pl.ds(k, 1), :] = jnp.full((1, LANES), place, jnp.int32)
            row = donor[e]
            block = jnp.where(row >= 8, 1, 0)
            inner = row - 8 * block
            ox = offset_x[e]
            oy = offset_y[e]
            fx = fraction_x[e]
            fy = fraction_y[e]
            half = oy >> 1
            odd = (oy & 1) == 1
            even_first = jnp.where(odd, 0.0, 1.0 - fy)
            even_second = jnp.where(odd, fy, 0.0)
            odd_weight = jnp.where(odd, 1.0 - fy, fy)
            near = column + ox < TILE
            far = column + ox + 1 < TILE
            for f in range(FIELDS):
                tile = cells[f, block, pl.ds(inner, CHUNKS, stride=8), :]
                first = pltpu.roll(tile, LANES - ox, 1)
                second = pltpu.roll(tile, LANES - 1 - ox, 1)
                first = jnp.where(near, first, pltpu.roll(first, TILE, 1))
                second = jnp.where(far, second, pltpu.roll(second, TILE, 1))
                mixed = (1.0 - fx) * first + fx * second
                swapped = pltpu.roll(mixed, TILE, 1)
                twice[0, f, 0:CHUNKS, :] = mixed
                twice[0, f, CHUNKS : 2 * CHUNKS, :] = mixed
                twice[1, f, 0:CHUNKS, :] = swapped
                twice[1, f, CHUNKS : 2 * CHUNKS, :] = swapped
            for f in range(FIELDS):
                here = twice[0, f, pl.ds(half, CHUNKS), :]
                after = twice[0, f, pl.ds(half + 1, CHUNKS), :]
                odd_here = twice[1, f, pl.ds(half, CHUNKS), :]
                odd_after = twice[1, f, pl.ds(half + 1, CHUNKS), :]
                packed[i, k, f] = (
                    even_first * here
                    + even_second * after
                    + odd_weight * jnp.where(low_half, odd_here, odd_after)
                )
            return inner_carry

        lax.fori_loop(0, CAP, one_slot, 0)

        @pl.when(i < planes - 1)
        def _():
            for copy in to_plane(i):
                copy.start()

        return carry

    landing[...] = jnp.full(landing.shape, -1, jnp.int32)
    lax.fori_loop(0, planes, fill, 0)
    own_tiles = pltpu.make_async_copy(packed.at[planes - 1], packed_in.at[p], own_sem.at[2])
    own_land = pltpu.make_async_copy(landing.at[planes - 1], landing_in.at[p], own_sem.at[3])
    own_tiles.start()
    own_land.start()

    for copy in large[1:]:
        copy.wait()
    spread(raw_coefs, coefs)

    def one_part(part, carry):
        eliminate(cells, coefs, solved, tips, part)
        return carry

    lax.fori_loop(0, CHUNKS // 8, one_part, 0)

    tip_copies = [to_azim(tips, tips_in, tip_rows, tips_send, tips_recv, o) for o in range(1, azims)]
    for copy in tip_copies:
        copy.start()
    own_tips = own_azim(tips, tips_in, tip_rows, 0)
    own_tips.start()
    own_tips.wait()
    for copy in tip_copies:
        copy.wait()

    for v in range(TIPS):
        value = tips_in[pl.ds(v, CHUNKS, stride=TIPS), :]
        ping[v, 0:CHUNKS, :] = value
        ping[v, CHUNKS : 2 * CHUNKS, :] = value

    source, dest = ping, pong
    step = 1
    while step < azims:

        def level(part, carry, source=source, dest=dest, shift=step * per):
            row = pl.multiple_of(part * 8, 8)
            left = [source[COLS * i : COLS * (i + 1), pl.ds(row, 8), :] for i in range(4)]
            right = [source[COLS * i : COLS * (i + 1), pl.ds(row + shift, 8), :] for i in range(4)]
            for i, value in enumerate(merge(left, right)):
                dest[COLS * i : COLS * (i + 1), pl.ds(row, 8), :] = value
                dest[COLS * i : COLS * (i + 1), pl.ds(row + CHUNKS, 8), :] = value
            return carry

        lax.fori_loop(0, CHUNKS // 8, level, 0)
        source, dest = dest, source
        step *= 2

    def last(part, carry):
        row = pl.multiple_of(part * 8, 8)
        block = [source[COLS * i : COLS * (i + 1), pl.ds(row, 8), :] for i in range(4)]
        values = close(block)
        for i in range(2):
            firsts[FIELDS * i : FIELDS * (i + 1), pl.ds(row, 8), :] = values[i]
            firsts[FIELDS * i : FIELDS * (i + 1), pl.ds(row + CHUNKS, 8), :] = values[i]
            for f in range(FIELDS):
                answers[pl.ds(part * 8 * BACK + i * FIELDS + f, 8, stride=BACK), :] = values[2 + i][f]
        return carry

    lax.fori_loop(0, CHUNKS // 8, last, 0)
    for v in range(2 * FIELDS):
        answers[pl.ds(2 * FIELDS + v, CHUNKS, stride=BACK), :] = firsts[v, per : per + CHUNKS, :]

    back_copies = [
        to_azim(answers, borders, back_rows, back_send, back_recv, o) for o in range(1, azims)
    ]
    for copy in back_copies:
        copy.start()
    own_back = own_azim(answers, borders, back_rows, 1)
    own_back.start()
    own_back.wait()
    for copy in back_copies:
        copy.wait()

    def compose(part, carry):
        at = pl.ds(pl.multiple_of(part * 8, 8), 8)

        def border(i, f):
            return borders[pl.ds(part * 8 * BACK + i * FIELDS + f, 8, stride=BACK), :]

        for f in range(FIELDS):
            outside = [border(i, f) for i in range(4)]
            for r in range(ROWS):
                value = solved[r, f, at, :]
                for i in range(4):
                    value = value - solved[r, FIELDS + i, at, :] * outside[i]
                cells[f, r // 8, pl.ds(part * 64 + r % 8, 8, stride=8), :] = value
        return carry

    lax.fori_loop(0, CHUNKS // 8, compose, 0)

    def move(c, carry):
        at = pl.ds(pl.multiple_of(c * LANES, LANES), LANES)
        row = pl.multiple_of(c * 8, 8)
        for f in range(FIELDS):
            update[f, 0:8, at] = cells[f, 0, pl.ds(row, 8), :] - state[f, 0:8, at]
            update[f, 8:12, at] = cells[f, 1, pl.ds(row, 4), :] - state[f, 8:12, at]
        return carry

    lax.fori_loop(0, CHUNKS, move, 0, unroll=4)

    own_tiles.wait()
    own_land.wait()

    def settle(i, carry):
        for copy in to_plane(i):
            copy.wait()
        return carry

    lax.fori_loop(0, planes - 1, settle, 0)


def finish_kernel(landing, packed, update, state, fringe, out_hbm, out, rows, cells, total, places, counts, sems):
    planes = landing.shape[0]
    fetch = pltpu.make_async_copy(landing, places, sems.at[FIELDS])
    fetch.start()
    for r in range(ROWS):
        counts[r] = 0.0
    total[...] = jnp.zeros(total.shape, jnp.float32)
    fetch.wait()

    def add(slot, carry):
        d = slot // CAP
        k = slot - d * CAP
        row = places[d, k, 0]

        @pl.when(row >= 0)
        def _():
            total[row] = total[row] + packed[d, k]
            counts[row] = counts[row] + 1.0

        return carry

    lax.fori_loop(0, planes * CAP, add, 0)

    for b in range(2):
        line = lax.broadcasted_iota(jnp.int32, (8, LANES), 0) + 8 * b
        number = jnp.zeros((8, LANES), jnp.float32)
        for r in range(8 * b, min(8 * b + 8, ROWS)):
            number = jnp.where(line == r, counts[r], number)
        rows[2 * b] = number
        rows[2 * b + 1] = 1.0 / (number + 1.0)

    copies = []
    for f in range(FIELDS):
        for r in range(ROWS):
            cells[r // 8, pl.ds(r % 8, CHUNKS, stride=8), :] = total[r, f]

        def move(c, carry, f=f):
            at = pl.ds(pl.multiple_of(c * LANES, LANES), LANES)
            row = pl.multiple_of(c * 8, 8)
            for b, (low, high) in enumerate(((0, 8), (8, ROWS))):
                size = high - low
                q = state[f, low:high, at]
                relaxed = (cells[b, pl.ds(row, size), :] - rows[2 * b, 0:size, :] * q) * rows[
                    2 * b + 1, 0:size, :
                ]
                out[f, low:high, at] = jnp.where(
                    fringe[low:high, at] == 1, relaxed, update[f, low:high, at]
                )
            return carry

        lax.fori_loop(0, CHUNKS, move, 0, unroll=4)
        copy = pltpu.make_async_copy(out.at[f], out_hbm.at[f], sems.at[f])
        copy.start()
        copies.append(copy)
    for copy in copies:
        copy.wait()


def f32(*shape):
    return jax.ShapeDtypeStruct(shape, jnp.float32)


def local(
    state,
    speed,
    sigma,
    dissipation,
    fringe,
    destination,
    donor,
    receptor,
    offset_y,
    offset_x,
    fraction_y,
    fraction_x,
):
    azims = lax.axis_size("azim")
    planes = lax.axis_size("plane")
    vmem = pl.BlockSpec(memory_space=pltpu.VMEM)
    hbm = pl.BlockSpec(memory_space=pltpu.HBM)
    number = pltpu.VMEM
    packed_in, landing_in, update = pl.pallas_call(
        functools.partial(exchange_kernel, azims, planes),
        out_shape=(
            f32(planes, CAP, FIELDS, CHUNKS, LANES),
            jax.ShapeDtypeStruct((planes, 8, LANES), jnp.int32),
            f32(FIELDS, ROWS, CELLS),
        ),
        in_specs=[hbm] * 11,
        out_specs=(vmem,) * 3,
        scratch_shapes=[pltpu.SMEM((SLOTS,), jnp.int32)] * 5
        + [pltpu.SMEM((SLOTS,), jnp.float32)] * 2
        + [
            pltpu.SMEM((CAP,), jnp.int32),
            number((FIELDS, ROWS, CELLS), jnp.float32),
            number((3, ROWS, CELLS), jnp.float32),
            number((FIELDS, 2, CHUNKS * 8, LANES), jnp.float32),
            number((3, 2, CHUNKS * 8, LANES), jnp.float32),
            number((2, FIELDS, 2 * CHUNKS, LANES), jnp.float32),
            number((planes, CAP, FIELDS, CHUNKS, LANES), jnp.float32),
            number((planes, 8, LANES), jnp.int32),
            number((ROWS, COLS, CHUNKS, LANES), jnp.float32),
            number((CHUNKS * TIPS, LANES), jnp.float32),
            number((CHUNKS * TIPS, LANES), jnp.float32),
            number((TIPS, 2 * CHUNKS, LANES), jnp.float32),
            number((TIPS, 2 * CHUNKS, LANES), jnp.float32),
            number((2 * FIELDS, 2 * CHUNKS, LANES), jnp.float32),
            number((CHUNKS * BACK, LANES), jnp.float32),
            number((CHUNKS * BACK, LANES), jnp.float32),
            pltpu.SemaphoreType.DMA((7,)),
            pltpu.SemaphoreType.DMA((4,)),
            pltpu.SemaphoreType.DMA((planes,)),
            pltpu.SemaphoreType.DMA((planes,)),
            pltpu.SemaphoreType.DMA((planes,)),
            pltpu.SemaphoreType.DMA((planes,)),
            pltpu.SemaphoreType.DMA((azims,)),
            pltpu.SemaphoreType.DMA((azims,)),
            pltpu.SemaphoreType.DMA((azims,)),
            pltpu.SemaphoreType.DMA((azims,)),
            pltpu.SemaphoreType.DMA((4,)),
        ],
        compiler_params=pltpu.CompilerParams(
            collective_id=0, has_side_effects=True, vmem_limit_bytes=40 * 2**20
        ),
        name="exchange",
    )(
        *(
            pltpu.with_memory_space_constraint(value, pltpu.HBM)
            for value in (
                destination.reshape(SLOTS),
                donor,
                receptor,
                offset_y,
                offset_x,
                fraction_y,
                fraction_x,
                state,
                speed,
                sigma,
                dissipation,
            )
        )
    )
    return pl.pallas_call(
        finish_kernel,
        out_shape=f32(FIELDS, ROWS, CELLS),
        in_specs=[vmem] * 5,
        out_specs=hbm,
        scratch_shapes=[
            number((FIELDS, ROWS, CELLS), jnp.float32),
            number((4, 8, LANES), jnp.float32),
            number((2, CHUNKS * 8, LANES), jnp.float32),
            number((ROWS, FIELDS, CHUNKS, LANES), jnp.float32),
            pltpu.SMEM((planes, 8, LANES), jnp.int32),
            pltpu.SMEM((ROWS,), jnp.float32),
            pltpu.SemaphoreType.DMA((FIELDS + 1,)),
        ],
        compiler_params=pltpu.CompilerParams(vmem_limit_bytes=32 * 2**20),
        name="finish",
    )(landing_in, packed_in, update, state, fringe)


def solution(mesh):
    in_specs = (
        P(None, "azim", "plane"),
        P("azim", "plane"),
        P("azim", "plane"),
        P("azim", "plane"),
        P("azim", "plane"),
        P(("azim", "plane"), None),
        P(("azim", "plane")),
        P(("azim", "plane")),
        P(("azim", "plane")),
        P(("azim", "plane")),
        P(("azim", "plane")),
        P(("azim", "plane")),
    )
    out_specs = P(None, "azim", "plane")
    return jax.shard_map(local, mesh=mesh, in_specs=in_specs, out_specs=out_specs, check_vma=False)
```

time: 59.9 us -> 46.7 us (0.78)
  local copies, waits for them, and re-layouts: 8.84 us -> 0.01 us
  Pallas kernels: 50.8 us -> 46.6 us
    unnamed x25 -> x4, local copies, waits for them, and re-layouts: 8.84 us -> 0.01 us
    pallas_call x1 -> x0, Pallas kernels: 6.27 us -> none  [local(): pl.pallas_call(prepare_kernel, out_shape=(f32(planes, CAP, FIELDS, CHUNKS...]
    pallas_call x1, Pallas kernels: 40.5 us -> 43 us  [local(): pl.pallas_call(functools.partial(exchange_kernel, azims, planes), out_sha...]
where the time goes in v1:
time: 46.7 us; the launch traced here: 46.6 us
  Pallas kernels  46.6 us (100%)
    pallas_call x1, Pallas kernels, local(): pl.pallas_call(functools.partial(exchange_kernel, azims, planes), out_sha...  43 us
    pallas_call x1, Pallas kernels, local(): pl.pallas_call(finish_kernel, out_shape=f32(FIELDS, ROWS, CELLS), in_spec...  3.6 us

profile of v1, /device:TPU:1, one launch (start us, length us, event | category | flops | bytes accessed | tf_op | source)
XLA Modules:
  0.0 46.6 jit_solution(11706172079359022201)
XLA Ops:
  0.0 0.0 copy-start
  0.0 0.0 copy-start.1
  0.0 43.0 %exchange.1 = (f32[8,4,5,32,128]{4,3,2,1,0:T(8,128)S(1)}, s32[8,8,128]{2,1,0:T(8,128)S(1)}, f32[5,12,4096]{2,1,0:T(8,128)S(1)}) custom-call(s32[16]{0:T(128)} %bitcast.1, s32[16]{0:T(128)} %donor_hbm.1, s32[16]{0:T(128)} %receptor_hbm.1, s32[16]{0:T(128)} %offset_y_hbm.1, s32[16]{0:T(128)} %offset_x_hbm.1, f32[16]{0:T(128)} %fraction_y_hbm.1, ...), custom_call_target="tpu_custom_call" | custom-call | tf_op jit(solution)/shard_map/exchange/pallas_call | solution.py:589
  43.0 0.0 copy-done
  43.0 0.0 copy-done.1
  43.0 3.6 %finish.1 = f32[5,12,4096]{2,1,0:T(8,128)} custom-call(s32[8,8,128]{2,1,0:T(8,128)S(1)} %get-tuple-element.8.landing, f32[8,4,5,32,128]{4,3,2,1,0:T(8,128)S(1)} %get-tuple-element.9.packed, f32[5,12,4096]{2,1,0:T(8,128)S(1)} %get-tuple-element.10.update, f32[5,12,4096]{2,1,0:T(8,128)S(1)} %copy-done, s32[12,4096]{1,0:T(8,128)S(1)} %copy-done.1), custom_call_target="tpu_custom_call" | custom-call | tf_op jit(solution)/shard_map/finish/pallas_call | solution.py:651
Async XLA Ops:
  0.0 43.0 %copy-start = (f32[5,12,4096]{2,1,0:T(8,128)S(1)}, f32[5,12,4096]{2,1,0:T(8,128)}, u32[]{:S(2)}) copy-start(f32[5,12,4096]{2,1,0:T(8,128)} %state.1) | copy-start | bytes 2949124
  0.0 43.0 %copy-start.1 = (s32[12,4096]{1,0:T(8,128)S(1)}, s32[12,4096]{1,0:T(8,128)}, u32[]{:S(2)}) copy-start(s32[12,4096]{1,0:T(8,128)} %fringe.1) | copy-start | bytes 589828

commit v2 on v1

--- a/solution.py
+++ b/solution.py
@@ -230,6 +230,8 @@
     back_send,
     back_recv,
     own_sem,
+    ready,
+    go,
 ):
     a = lax.axis_index("azim")
     p = lax.axis_index("plane")
@@ -270,13 +272,11 @@
 
     barrier = pltpu.get_barrier_semaphore()
     for o in range(1, planes):
-        pl.semaphore_signal(
-            barrier, inc=1, device_id=(a, lax.rem(p + o, planes)), device_id_type=MESH
-        )
-    for o in range(1, azims):
-        pl.semaphore_signal(
-            barrier, inc=1, device_id=(lax.rem(a + o, azims), p), device_id_type=MESH
-        )
+        there = lax.rem(p + o, planes)
+
+        @pl.when(there != 0)
+        def _():
+            pl.semaphore_signal(barrier, inc=1, device_id=(a, there), device_id_type=MESH)
 
     def to_azim(source, dest, rows, send, recv, o):
         there = lax.rem(a + o, azims)
@@ -327,7 +327,20 @@
         copy.wait()
     large[0].wait()
     spread(state, cells)
-    pl.semaphore_wait(barrier, planes + azims - 2)
+
+    @pl.when(p != 0)
+    def _():
+        pl.semaphore_wait(barrier, planes - 1)
+        pl.semaphore_signal(ready, inc=1, device_id=(a, 0), device_id_type=MESH)
+
+    @pl.when(p == 0)
+    def _():
+        pl.semaphore_wait(ready, planes - 1)
+        for o in range(1, azims):
+            pl.semaphore_signal(
+                barrier, inc=1, device_id=(lax.rem(a + o, azims), p), device_id_type=MESH
+            )
+
 
     def fill(i, carry):
         target = plane_peer(i)
@@ -409,6 +422,16 @@
         return carry
 
     lax.fori_loop(0, CHUNKS // 8, one_part, 0)
+
+    @pl.when(p == 0)
+    def _():
+        pl.semaphore_wait(barrier, azims - 1)
+        for o in range(1, planes):
+            pl.semaphore_signal(go, inc=1, device_id=(a, o), device_id_type=MESH)
+
+    @pl.when(p != 0)
+    def _():
+        pl.semaphore_wait(go, 1)
 
     tip_copies = [to_azim(tips, tips_in, tip_rows, tips_send, tips_recv, o) for o in range(1, azims)]
     for copy in tip_copies:
@@ -625,6 +648,8 @@
             pltpu.SemaphoreType.DMA((azims,)),
             pltpu.SemaphoreType.DMA((azims,)),
             pltpu.SemaphoreType.DMA((4,)),
+            pltpu.SemaphoreType.REGULAR,
+            pltpu.SemaphoreType.REGULAR,
         ],
         compiler_params=pltpu.CompilerParams(
             collective_id=0, has_side_effects=True, vmem_limit_bytes=40 * 2**20

time: 46.7 us -> 42.1 us (0.901)
  Pallas kernels: 46.6 us -> 41.8 us
    pallas_call x1, Pallas kernels: 43 us -> 38.3 us  [local(): pl.pallas_call(functools.partial(exchange_kernel, azims, planes), out_sha...]
where the time goes in v2:
time: 42.1 us; the launch traced here: 41.8 us
  Pallas kernels  41.8 us (99%)
    pallas_call x1, Pallas kernels, local(): pl.pallas_call(functools.partial(exchange_kernel, azims, planes), out_sha...  38.3 us
    pallas_call x1, Pallas kernels, local(): pl.pallas_call(finish_kernel, out_shape=f32(FIELDS, ROWS, CELLS), in_spec...  3.48 us

profile of v2, /device:TPU:1, one launch (start us, length us, event | category | flops | bytes accessed | tf_op | source)
XLA Modules:
  0.0 41.8 jit_solution(16812561490953209265)
XLA Ops:
  0.0 0.0 copy-start
  0.0 0.0 copy-start.1
  0.0 38.3 %exchange.1 = (f32[8,4,5,32,128]{4,3,2,1,0:T(8,128)S(1)}, s32[8,8,128]{2,1,0:T(8,128)S(1)}, f32[5,12,4096]{2,1,0:T(8,128)S(1)}) custom-call(s32[16]{0:T(128)} %bitcast.1, s32[16]{0:T(128)} %donor_hbm.1, s32[16]{0:T(128)} %receptor_hbm.1, s32[16]{0:T(128)} %offset_y_hbm.1, s32[16]{0:T(128)} %offset_x_hbm.1, f32[16]{0:T(128)} %fraction_y_hbm.1, ...), custom_call_target="tpu_custom_call" | custom-call | tf_op jit(solution)/shard_map/exchange/pallas_call | solution.py:612
  38.3 0.0 copy-done
  38.3 0.0 copy-done.1
  38.3 3.5 %finish.1 = f32[5,12,4096]{2,1,0:T(8,128)} custom-call(s32[8,8,128]{2,1,0:T(8,128)S(1)} %get-tuple-element.8.landing, f32[8,4,5,32,128]{4,3,2,1,0:T(8,128)S(1)} %get-tuple-element.9.packed, f32[5,12,4096]{2,1,0:T(8,128)S(1)} %get-tuple-element.10.update, f32[5,12,4096]{2,1,0:T(8,128)S(1)} %copy-done, s32[12,4096]{1,0:T(8,128)S(1)} %copy-done.1), custom_call_target="tpu_custom_call" | custom-call | tf_op jit(solution)/shard_map/finish/pallas_call | solution.py:676
Async XLA Ops:
  0.0 38.3 %copy-start = (f32[5,12,4096]{2,1,0:T(8,128)S(1)}, f32[5,12,4096]{2,1,0:T(8,128)}, u32[]{:S(2)}) copy-start(f32[5,12,4096]{2,1,0:T(8,128)} %state.1) | copy-start | bytes 2949124
  0.0 38.3 %copy-start.1 = (s32[12,4096]{1,0:T(8,128)S(1)}, s32[12,4096]{1,0:T(8,128)}, u32[]{:S(2)}) copy-start(s32[12,4096]{1,0:T(8,128)} %fringe.1) | copy-start | bytes 589828

commit v3 on v2

--- a/solution.py
+++ b/solution.py
@@ -32,6 +32,20 @@
         return carry
 
     lax.fori_loop(0, CHUNKS, move, 0, unroll=4)
+
+
+def spread_twice(source, dest):
+    def move(c, carry):
+        lane = pl.multiple_of(c * LANES, LANES)
+        row = pl.multiple_of(c * 8, 8)
+        upper = source[0:8, pl.ds(lane, LANES)]
+        lower = source[8:12, pl.ds(lane, LANES)]
+        for again in range(2):
+            dest[0, pl.ds(row + again * CHUNKS * 8, 8), :] = upper
+            dest[1, pl.ds(row + again * CHUNKS * 8, 4), :] = lower
+        return carry
+
+    lax.fori_loop(0, CHUNKS, move, 0, unroll=8)
 
 
 def eliminate(cells, coefs, solved, tips, part):
@@ -208,7 +222,6 @@
     raw_coefs,
     cells,
     coefs,
-    twice,
     packed,
     landing,
     solved,
@@ -231,6 +244,7 @@
     back_recv,
     own_sem,
     ready,
+    beyond,
     go,
 ):
     a = lax.axis_index("azim")
@@ -257,12 +271,12 @@
     large = [
         pltpu.make_async_copy(source, dest, large_sem.at[i])
         for i, (source, dest) in enumerate(
-            (
-                (state_hbm, state),
+            [(state_hbm.at[f], state.at[f]) for f in range(FIELDS)]
+            + [
                 (speed_hbm, raw_coefs.at[0]),
                 (sigma_hbm, raw_coefs.at[1]),
                 (dissipation_hbm, raw_coefs.at[2]),
-            )
+            ]
         )
     ]
     for copy in small:
@@ -271,8 +285,14 @@
         copy.start()
 
     barrier = pltpu.get_barrier_semaphore()
-    for o in range(1, planes):
-        there = lax.rem(p + o, planes)
+    near = [(0, 1), (1, 0), (1, 1), (chips - 1, 0), (chips - 1, 1)]
+    leader = p == 0
+
+    def plane_at(ahead, flip):
+        return lax.rem(p // 2 + ahead, chips) * 2 + lax.rem(p + flip, 2)
+
+    for ahead, flip in near:
+        there = plane_at(ahead, flip)
 
         @pl.when(there != 0)
         def _():
@@ -294,9 +314,12 @@
         return pltpu.make_async_copy(source.at[at, :], dest.at[at, :], own_sem.at[index])
 
     def plane_peer(i):
-        chip = lax.rem(p // 2 + chips - 1 - lax.rem(i, chips), chips)
-        core = lax.rem(p + 1 - i // chips, 2)
-        return chip * 2 + core
+        late = i // 4
+        pair = i // 2 - 2 * late
+        odd = i - 2 * (i // 2)
+        ahead = (1 - late) * (chips - 1 - (chips - 2) * odd) + late * (chips // 2) * (1 - pair)
+        flip = (1 - late) * (1 - pair) + late * (1 - odd)
+        return plane_at(ahead, flip)
 
     def to_plane(i):
         there = plane_peer(i)
@@ -320,29 +343,13 @@
         )
 
     lane = lax.broadcasted_iota(jnp.int32, (CHUNKS, LANES), 1)
-    column = lane & (TILE - 1)
-    low_half = lane < TILE
+    high_half = lane >= TILE
+    spot = lax.broadcasted_iota(jnp.int32, (1, LANES), 1)
 
     for copy in small:
         copy.wait()
-    large[0].wait()
-    spread(state, cells)
-
-    @pl.when(p != 0)
-    def _():
-        pl.semaphore_wait(barrier, planes - 1)
-        pl.semaphore_signal(ready, inc=1, device_id=(a, 0), device_id_type=MESH)
-
-    @pl.when(p == 0)
-    def _():
-        pl.semaphore_wait(ready, planes - 1)
-        for o in range(1, azims):
-            pl.semaphore_signal(
-                barrier, inc=1, device_id=(lax.rem(a + o, azims), p), device_id_type=MESH
-            )
-
-
-    def fill(i, carry):
+
+    def search(i, carry):
         target = plane_peer(i)
         seen = jnp.int32(0)
         found = [jnp.int32(-1)] * CAP
@@ -352,52 +359,73 @@
                 found[k] = jnp.where(match & (seen == k), e, found[k])
             seen = seen + jnp.where(match, 1, 0)
         for k in range(CAP):
-            entries[k] = found[k]
-
-        def one_slot(k, inner_carry):
-            entry = entries[k]
+            entries[i * CAP + k] = found[k]
+        return carry
+
+    lax.fori_loop(0, planes, search, 0)
+    for f in range(FIELDS):
+        large[f].wait()
+        spread_twice(state.at[f], cells.at[f])
+
+    @pl.when(jnp.logical_not(leader))
+    def _():
+        pl.semaphore_wait(barrier, len(near))
+
+    @pl.when(jnp.logical_not(leader) & (p // 2 != chips // 2))
+    def _():
+        pl.semaphore_signal(ready, inc=1, device_id=(a, 0), device_id_type=MESH)
+
+    @pl.when(leader)
+    def _():
+        pl.semaphore_wait(ready, len(near))
+
+    for ahead in (1, chips - 1):
+        pl.semaphore_signal(beyond, inc=1, device_id=(a, plane_at(ahead, 0)), device_id_type=MESH)
+
+    wide = lax.broadcasted_iota(jnp.int32, (LANES, 2 * LANES), 1)
+    second = wide // LANES
+    wide_lane = wide & (LANES - 1)
+    from_lane = lax.broadcasted_iota(jnp.int32, (LANES, 2 * LANES), 0)
+
+    def fill(i, carry):
+        places = jnp.full((1, LANES), -1, jnp.int32)
+        for k in range(CAP):
+            entry = entries[i * CAP + k]
             e = jnp.maximum(entry, 0)
-            place = jnp.where(entry >= 0, receptor[e], -1)
-            landing[i, pl.ds(k, 1), :] = jnp.full((1, LANES), place, jnp.int32)
+            places = jnp.where(spot == k, jnp.where(entry >= 0, receptor[e], -1), places)
             row = donor[e]
             block = jnp.where(row >= 8, 1, 0)
-            inner = row - 8 * block
             ox = offset_x[e]
             oy = offset_y[e]
             fx = fraction_x[e]
             fy = fraction_y[e]
-            half = oy >> 1
+            start = row - 8 * block + 8 * (oy >> 1)
             odd = (oy & 1) == 1
             even_first = jnp.where(odd, 0.0, 1.0 - fy)
             even_second = jnp.where(odd, fy, 0.0)
             odd_weight = jnp.where(odd, 1.0 - fy, fy)
-            near = column + ox < TILE
-            far = column + ox + 1 < TILE
+            pick = (wide_lane & TILE) + ((wide_lane + ox + second) & (TILE - 1))
+            chosen = jnp.where(from_lane == pick, 1.0, 0.0).astype(jnp.bfloat16)
+            values = []
             for f in range(FIELDS):
-                tile = cells[f, block, pl.ds(inner, CHUNKS, stride=8), :]
-                first = pltpu.roll(tile, LANES - ox, 1)
-                second = pltpu.roll(tile, LANES - 1 - ox, 1)
-                first = jnp.where(near, first, pltpu.roll(first, TILE, 1))
-                second = jnp.where(far, second, pltpu.roll(second, TILE, 1))
-                mixed = (1.0 - fx) * first + fx * second
-                swapped = pltpu.roll(mixed, TILE, 1)
-                twice[0, f, 0:CHUNKS, :] = mixed
-                twice[0, f, CHUNKS : 2 * CHUNKS, :] = mixed
-                twice[1, f, 0:CHUNKS, :] = swapped
-                twice[1, f, CHUNKS : 2 * CHUNKS, :] = swapped
+                here = cells[f, block, pl.ds(start, CHUNKS, stride=8), :]
+                after = cells[f, block, pl.ds(start + 8, CHUNKS, stride=8), :]
+                between = pltpu.roll(jnp.where(high_half, here, after), TILE, 1)
+                values.append(even_first * here + even_second * after + odd_weight * between)
+            value = jnp.concatenate(values, axis=0)
+            high = value.astype(jnp.bfloat16)
+            rest = value - high.astype(jnp.float32)
+            middle = rest.astype(jnp.bfloat16)
+            low = (rest - middle.astype(jnp.float32)).astype(jnp.bfloat16)
+            moved = jnp.dot(
+                jnp.concatenate([high, middle, low], axis=1),
+                jnp.concatenate([chosen, chosen, chosen], axis=0),
+                preferred_element_type=jnp.float32,
+            )
+            mixed = (1.0 - fx) * moved[:, :LANES] + fx * moved[:, LANES:]
             for f in range(FIELDS):
-                here = twice[0, f, pl.ds(half, CHUNKS), :]
-                after = twice[0, f, pl.ds(half + 1, CHUNKS), :]
-                odd_here = twice[1, f, pl.ds(half, CHUNKS), :]
-                odd_after = twice[1, f, pl.ds(half + 1, CHUNKS), :]
-                packed[i, k, f] = (
-                    even_first * here
-                    + even_second * after
-                    + odd_weight * jnp.where(low_half, odd_here, odd_after)
-                )
-            return inner_carry
-
-        lax.fori_loop(0, CAP, one_slot, 0)
+                packed[i, k, f] = mixed[f * CHUNKS : (f + 1) * CHUNKS]
+        landing[i] = places
 
         @pl.when(i < planes - 1)
         def _():
@@ -406,14 +434,23 @@
 
         return carry
 
-    landing[...] = jnp.full(landing.shape, -1, jnp.int32)
-    lax.fori_loop(0, planes, fill, 0)
+    lax.fori_loop(0, planes // 2, fill, 0)
+    pl.semaphore_wait(beyond, 2)
+
+    @pl.when(leader)
+    def _():
+        for o in range(1, azims):
+            pl.semaphore_signal(
+                barrier, inc=1, device_id=(lax.rem(a + o, azims), p), device_id_type=MESH
+            )
+
+    lax.fori_loop(planes // 2, planes, fill, 0)
     own_tiles = pltpu.make_async_copy(packed.at[planes - 1], packed_in.at[p], own_sem.at[2])
     own_land = pltpu.make_async_copy(landing.at[planes - 1], landing_in.at[p], own_sem.at[3])
     own_tiles.start()
     own_land.start()
 
-    for copy in large[1:]:
+    for copy in large[FIELDS:]:
         copy.wait()
     spread(raw_coefs, coefs)
 
@@ -423,13 +460,13 @@
 
     lax.fori_loop(0, CHUNKS // 8, one_part, 0)
 
-    @pl.when(p == 0)
+    @pl.when(leader)
     def _():
         pl.semaphore_wait(barrier, azims - 1)
         for o in range(1, planes):
             pl.semaphore_signal(go, inc=1, device_id=(a, o), device_id_type=MESH)
 
-    @pl.when(p != 0)
+    @pl.when(jnp.logical_not(leader))
     def _():
         pl.semaphore_wait(go, 1)
 
@@ -540,7 +577,7 @@
     def add(slot, carry):
         d = slot // CAP
         k = slot - d * CAP
-        row = places[d, k, 0]
+        row = places[d, 0, k]
 
         @pl.when(row >= 0)
         def _():
@@ -613,7 +650,7 @@
         functools.partial(exchange_kernel, azims, planes),
         out_shape=(
             f32(planes, CAP, FIELDS, CHUNKS, LANES),
-            jax.ShapeDtypeStruct((planes, 8, LANES), jnp.int32),
+            jax.ShapeDtypeStruct((planes, 1, LANES), jnp.int32),
             f32(FIELDS, ROWS, CELLS),
         ),
         in_specs=[hbm] * 11,
@@ -621,14 +658,13 @@
         scratch_shapes=[pltpu.SMEM((SLOTS,), jnp.int32)] * 5
         + [pltpu.SMEM((SLOTS,), jnp.float32)] * 2
         + [
-            pltpu.SMEM((CAP,), jnp.int32),
+            pltpu.SMEM((planes * CAP,), jnp.int32),
             number((FIELDS, ROWS, CELLS), jnp.float32),
             number((3, ROWS, CELLS), jnp.float32),
-            number((FIELDS, 2, CHUNKS * 8, LANES), jnp.float32),
+            number((FIELDS, 2, 2 * CHUNKS * 8, LANES), jnp.float32),
             number((3, 2, CHUNKS * 8, LANES), jnp.float32),
-            number((2, FIELDS, 2 * CHUNKS, LANES), jnp.float32),
             number((planes, CAP, FIELDS, CHUNKS, LANES), jnp.float32),
-            number((planes, 8, LANES), jnp.int32),
+            number((planes, 1, LANES), jnp.int32),
             number((ROWS, COLS, CHUNKS, LANES), jnp.float32),
             number((CHUNKS * TIPS, LANES), jnp.float32),
             number((CHUNKS * TIPS, LANES), jnp.float32),
@@ -638,7 +674,7 @@
             number((CHUNKS * BACK, LANES), jnp.float32),
             number((CHUNKS * BACK, LANES), jnp.float32),
             pltpu.SemaphoreType.DMA((7,)),
-            pltpu.SemaphoreType.DMA((4,)),
+            pltpu.SemaphoreType.DMA((FIELDS + 3,)),
             pltpu.SemaphoreType.DMA((planes,)),
             pltpu.SemaphoreType.DMA((planes,)),
             pltpu.SemaphoreType.DMA((planes,)),
@@ -648,6 +684,7 @@
             pltpu.SemaphoreType.DMA((azims,)),
             pltpu.SemaphoreType.DMA((azims,)),
             pltpu.SemaphoreType.DMA((4,)),
+            pltpu.SemaphoreType.REGULAR,
             pltpu.SemaphoreType.REGULAR,
             pltpu.SemaphoreType.REGULAR,
         ],
@@ -683,7 +720,7 @@
             number((4, 8, LANES), jnp.float32),
             number((2, CHUNKS * 8, LANES), jnp.float32),
             number((ROWS, FIELDS, CHUNKS, LANES), jnp.float32),
-            pltpu.SMEM((planes, 8, LANES), jnp.int32),
+            pltpu.SMEM((planes, 1, LANES), jnp.int32),
             pltpu.SMEM((ROWS,), jnp.float32),
             pltpu.SemaphoreType.DMA((FIELDS + 1,)),
         ],

time: 42.1 us -> 39.2 us (0.931)
  Pallas kernels: 41.8 us -> 39.1 us
    pallas_call x1, Pallas kernels: 38.3 us -> 36 us  [local(): pl.pallas_call(functools.partial(exchange_kernel, azims, planes), out_sha...]
    pallas_call x1, Pallas kernels: 3.48 us -> 3.04 us  [local(): pl.pallas_call(finish_kernel, out_shape=f32(FIELDS, ROWS, CELLS), in_spec...]
where the time goes in v3:
time: 39.2 us; the launch traced here: 39.1 us
  Pallas kernels  39.1 us (100%)
    pallas_call x1, Pallas kernels, local(): pl.pallas_call(functools.partial(exchange_kernel, azims, planes), out_sha...  36 us
    pallas_call x1, Pallas kernels, local(): pl.pallas_call(finish_kernel, out_shape=f32(FIELDS, ROWS, CELLS), in_spec...  3.04 us

profile of v3, /device:TPU:1, one launch (start us, length us, event | category | flops | bytes accessed | tf_op | source)
XLA Modules:
  0.0 39.1 jit_solution(11890959075151621451)
XLA Ops:
  0.0 0.0 copy-start
  0.0 0.0 copy-start.1
  0.0 36.0 %exchange.1 = (f32[8,4,5,32,128]{4,3,2,1,0:T(8,128)S(1)}, s32[8,1,128]{2,1,0:T(1,128)S(1)}, f32[5,12,4096]{2,1,0:T(8,128)S(1)}) custom-call(s32[16]{0:T(128)} %bitcast.1, s32[16]{0:T(128)} %donor_hbm.1, s32[16]{0:T(128)} %receptor_hbm.1, s32[16]{0:T(128)} %offset_y_hbm.1, s32[16]{0:T(128)} %offset_x_hbm.1, f32[16]{0:T(128)} %fraction_y_hbm.1, ...), custom_call_target="tpu_custom_call" | custom-call | tf_op jit(solution)/shard_map/exchange/pallas_call | solution.py:649
  36.1 0.0 copy-done
  36.1 0.0 copy-done.1
  36.1 3.0 %finish.1 = f32[5,12,4096]{2,1,0:T(8,128)} custom-call(s32[8,1,128]{2,1,0:T(1,128)S(1)} %get-tuple-element.8.landing, f32[8,4,5,32,128]{4,3,2,1,0:T(8,128)S(1)} %get-tuple-element.9.packed, f32[5,12,4096]{2,1,0:T(8,128)S(1)} %get-tuple-element.10.update, f32[5,12,4096]{2,1,0:T(8,128)S(1)} %copy-done, s32[12,4096]{1,0:T(8,128)S(1)} %copy-done.1), custom_call_target="tpu_custom_call" | custom-call | tf_op jit(solution)/shard_map/finish/pallas_call | solution.py:713
Async XLA Ops:
  0.0 36.1 %copy-start = (f32[5,12,4096]{2,1,0:T(8,128)S(1)}, f32[5,12,4096]{2,1,0:T(8,128)}, u32[]{:S(2)}) copy-start(f32[5,12,4096]{2,1,0:T(8,128)} %state.1) | copy-start | bytes 2949124
  0.0 36.1 %copy-start.1 = (s32[12,4096]{1,0:T(8,128)S(1)}, s32[12,4096]{1,0:T(8,128)}, u32[]{:S(2)}) copy-start(s32[12,4096]{1,0:T(8,128)} %fringe.1) | copy-start | bytes 589828

commit v4 on v3

--- a/solution.py
+++ b/solution.py
@@ -19,6 +19,9 @@
 TIPS = 4 * COLS
 BACK = 4 * FIELDS
 MESH = pl.DeviceIdType.MESH
+GROUPS = ((0, 3), (3, FIELDS))
+PLACES = 8
+SPREAD = CHUNKS * ROWS
 TIP_ROW = {0: 0, 1: 1, ROWS - 2: 2, ROWS - 1: 3}
 
 
@@ -35,17 +38,17 @@
 
 
 def spread_twice(source, dest):
-    def move(c, carry):
-        lane = pl.multiple_of(c * LANES, LANES)
-        row = pl.multiple_of(c * 8, 8)
-        upper = source[0:8, pl.ds(lane, LANES)]
-        lower = source[8:12, pl.ds(lane, LANES)]
-        for again in range(2):
-            dest[0, pl.ds(row + again * CHUNKS * 8, 8), :] = upper
-            dest[1, pl.ds(row + again * CHUNKS * 8, 4), :] = lower
+    def move(j, carry):
+        lane = pl.multiple_of(j * 2 * LANES, 2 * LANES)
+        row = pl.multiple_of(j * 2 * ROWS, 8)
+        value = jnp.concatenate(
+            [source[:, pl.ds(lane, LANES)], source[:, pl.ds(lane + LANES, LANES)]], axis=0
+        )
+        dest[pl.ds(row, 2 * ROWS), :] = value
+        dest[pl.ds(row + SPREAD, 2 * ROWS), :] = value
         return carry
 
-    lax.fori_loop(0, CHUNKS, move, 0, unroll=8)
+    lax.fori_loop(0, CHUNKS // 2, move, 0, unroll=4)
 
 
 def eliminate(cells, coefs, solved, tips, part):
@@ -54,6 +57,9 @@
 
     def load(ref, lead, r):
         return ref[lead, r // 8, pl.ds(base + r % 8, 8, stride=8), :]
+
+    def load_cells(k, r):
+        return cells[k, pl.ds(part * 8 * ROWS + r, 8, stride=ROWS), :]
 
     upper1 = []
     upper2 = []
@@ -83,7 +89,7 @@
         now = []
         for k in range(FIELDS + 2):
             if k < FIELDS:
-                value = weight * load(cells, k, r)
+                value = weight * load_cells(k, r)
             elif r == 0:
                 now.append((d if k == FIELDS else a1) * inverse)
                 continue
@@ -207,7 +213,8 @@
     speed_hbm,
     sigma_hbm,
     dissipation_hbm,
-    packed_in,
+    arrived0,
+    arrived1,
     landing_in,
     update,
     destination,
@@ -218,12 +225,22 @@
     fraction_y,
     fraction_x,
     entries,
+    integers,
+    reals,
     state,
     raw_coefs,
+    result,
     cells,
+    cells0,
+    cells1,
     coefs,
-    packed,
+    packed0,
+    packed1,
     landing,
+    integers_out,
+    reals_out,
+    integers_in,
+    reals_in,
     solved,
     tips,
     tips_in,
@@ -234,6 +251,11 @@
     borders,
     small_sem,
     large_sem,
+    raw_send,
+    raw_recv,
+    table_send,
+    table_recv,
+    table_sem,
     tile_send,
     tile_recv,
     land_send,
@@ -253,6 +275,11 @@
     tip_rows = per * TIPS
     back_rows = per * BACK
     chips = planes // 2
+    core = lax.rem(p, 2)
+    groups = (0, 1)
+    arrived = (arrived0, arrived1)
+    packed = (packed0, packed1)
+    raw_cells = (cells0, cells1)
 
     small = [
         pltpu.make_async_copy(source, dest, small_sem.at[i])
@@ -291,6 +318,19 @@
     def plane_at(ahead, flip):
         return lax.rem(p // 2 + ahead, chips) * 2 + lax.rem(p + flip, 2)
 
+    def remote(source, dest, send, recv, there):
+        return pltpu.make_async_remote_copy(
+            src_ref=source,
+            dst_ref=dest,
+            send_sem=send,
+            recv_sem=recv,
+            device_id=(a, there),
+            device_id_type=MESH,
+        )
+
+    onward = (1 + core * (chips - 2), chips - 1 - core * (chips - 2))
+    behind = (onward[1], onward[0])
+
     for ahead, flip in near:
         there = plane_at(ahead, flip)
 
@@ -313,93 +353,127 @@
         at = pl.ds(pl.multiple_of(a * rows, 8), rows)
         return pltpu.make_async_copy(source.at[at, :], dest.at[at, :], own_sem.at[index])
 
-    def plane_peer(i):
-        late = i // 4
-        pair = i // 2 - 2 * late
-        odd = i - 2 * (i // 2)
-        ahead = (1 - late) * (chips - 1 - (chips - 2) * odd) + late * (chips // 2) * (1 - pair)
-        flip = (1 - late) * (1 - pair) + late * (1 - odd)
-        return plane_at(ahead, flip)
-
-    def to_plane(i):
-        there = plane_peer(i)
+    def raw_copy(g):
+        low, high = GROUPS[g]
+        return remote(
+            cells.at[low:high, 0:SPREAD, :],
+            raw_cells[g].at[:, 0:SPREAD, :],
+            raw_send.at[g],
+            raw_recv.at[g],
+            plane_at(onward[g], 0),
+        )
+
+    def table_copies(g):
+        there = plane_at(onward[g], 0)
         return (
-            pltpu.make_async_remote_copy(
-                src_ref=packed.at[i],
-                dst_ref=packed_in.at[p],
-                send_sem=tile_send.at[i],
-                recv_sem=tile_recv.at[i],
-                device_id=(a, there),
-                device_id_type=MESH,
+            remote(integers_out, integers_in.at[g], table_send.at[2 * g], table_recv.at[2 * g], there),
+            remote(
+                reals_out, reals_in.at[g], table_send.at[2 * g + 1], table_recv.at[2 * g + 1], there
             ),
-            pltpu.make_async_remote_copy(
-                src_ref=landing.at[i],
-                dst_ref=landing_in.at[p],
-                send_sem=land_send.at[i],
-                recv_sem=land_recv.at[i],
-                device_id=(a, there),
-                device_id_type=MESH,
-            ),
-        )
-
-    lane = lax.broadcasted_iota(jnp.int32, (CHUNKS, LANES), 1)
-    high_half = lane >= TILE
+        )
+
+    def tile_copy(g, place, owner, ahead, flip):
+        index = g * PLACES + place
+        return remote(
+            packed[g].at[place],
+            arrived[g].at[owner],
+            tile_send.at[index],
+            tile_recv.at[index],
+            plane_at(ahead, flip),
+        )
+
+    def land_copy(index, owner, ahead, flip):
+        return remote(
+            landing.at[index],
+            landing_in.at[owner],
+            land_send.at[index],
+            land_recv.at[index],
+            plane_at(ahead, flip),
+        )
+
+    def direct_copy(g, flip):
+        return tile_copy(g, flip, p, behind[g], flip)
+
+    def relay_copy(g, u):
+        return tile_copy(g, 2 + u, plane_at(behind[g], 0), (1 - u // 2) * onward[g], u - 2 * (u // 2))
+
+    def mate_copy(g):
+        return tile_copy(g, 6, p, 0, 1)
+
     spot = lax.broadcasted_iota(jnp.int32, (1, LANES), 1)
-
     for copy in small:
         copy.wait()
-
-    def search(i, carry):
-        target = plane_peer(i)
+    for line, source in enumerate((destination, donor, receptor, offset_y, offset_x)):
+        value = jnp.zeros((1, LANES), jnp.int32)
+        for e in range(SLOTS):
+            value = jnp.where(spot == e, source[e], value)
+        integers_out[line : line + 1, :] = value
+    for line, source in enumerate((fraction_y, fraction_x)):
+        value = jnp.zeros((1, LANES), jnp.float32)
+        for e in range(SLOTS):
+            value = jnp.where(spot == e, source[e], value)
+        reals_out[line : line + 1, :] = value
+
+    for f in range(FIELDS):
+        large[f].wait()
+        spread_twice(state.at[f], cells.at[f])
+
+    @pl.when(jnp.logical_not(leader))
+    def _():
+        pl.semaphore_wait(barrier, len(near))
+
+    @pl.when(jnp.logical_not(leader) & (p // 2 != chips // 2))
+    def _():
+        pl.semaphore_signal(ready, inc=1, device_id=(a, 0), device_id_type=MESH)
+
+    @pl.when(leader)
+    def _():
+        pl.semaphore_wait(ready, len(near))
+
+    for g in groups:
+        for copy in table_copies(g):
+            copy.start()
+    for g in groups:
+        raw_copy(g).start()
+    for ahead in (1, chips - 1):
+        pl.semaphore_signal(beyond, inc=1, device_id=(a, plane_at(ahead, 0)), device_id_type=MESH)
+
+    def search(named, target, base):
         seen = jnp.int32(0)
         found = [jnp.int32(-1)] * CAP
         for e in range(SLOTS):
-            match = destination[e] == target
+            match = named(e) == target
             for k in range(CAP):
                 found[k] = jnp.where(match & (seen == k), e, found[k])
             seen = seen + jnp.where(match, 1, 0)
         for k in range(CAP):
-            entries[i * CAP + k] = found[k]
-        return carry
-
-    lax.fori_loop(0, planes, search, 0)
-    for f in range(FIELDS):
-        large[f].wait()
-        spread_twice(state.at[f], cells.at[f])
-
-    @pl.when(jnp.logical_not(leader))
-    def _():
-        pl.semaphore_wait(barrier, len(near))
-
-    @pl.when(jnp.logical_not(leader) & (p // 2 != chips // 2))
-    def _():
-        pl.semaphore_signal(ready, inc=1, device_id=(a, 0), device_id_type=MESH)
-
-    @pl.when(leader)
-    def _():
-        pl.semaphore_wait(ready, len(near))
-
-    for ahead in (1, chips - 1):
-        pl.semaphore_signal(beyond, inc=1, device_id=(a, plane_at(ahead, 0)), device_id_type=MESH)
-
+            entries[base + k] = found[k]
+
+    lane = lax.broadcasted_iota(jnp.int32, (CHUNKS, LANES), 1)
+    high_half = lane >= TILE
     wide = lax.broadcasted_iota(jnp.int32, (LANES, 2 * LANES), 1)
     second = wide // LANES
     wide_lane = wide & (LANES - 1)
     from_lane = lax.broadcasted_iota(jnp.int32, (LANES, 2 * LANES), 0)
 
-    def fill(i, carry):
+    def places_of(base, receptor_of):
         places = jnp.full((1, LANES), -1, jnp.int32)
         for k in range(CAP):
-            entry = entries[i * CAP + k]
-            e = jnp.maximum(entry, 0)
-            places = jnp.where(spot == k, jnp.where(entry >= 0, receptor[e], -1), places)
-            row = donor[e]
-            block = jnp.where(row >= 8, 1, 0)
-            ox = offset_x[e]
-            oy = offset_y[e]
-            fx = fraction_x[e]
-            fy = fraction_y[e]
-            start = row - 8 * block + 8 * (oy >> 1)
+            entry = entries[base + k]
+            place = jnp.where(entry >= 0, receptor_of(jnp.maximum(entry, 0)), -1)
+            places = jnp.where(spot == k, place, places)
+        return places
+
+    def fill(base, table, blocks, dests):
+        donor_of, oy_of, ox_of, fy_of, fx_of = table
+        for k in range(CAP):
+            e = jnp.maximum(entries[base + k], 0)
+            row = donor_of(e)
+            ox = ox_of(e)
+            oy = oy_of(e)
+            fx = fx_of(e)
+            fy = fy_of(e)
+            start = row + ROWS * (oy >> 1)
             odd = (oy & 1) == 1
             even_first = jnp.where(odd, 0.0, 1.0 - fy)
             even_second = jnp.where(odd, fy, 0.0)
@@ -407,9 +481,9 @@
             pick = (wide_lane & TILE) + ((wide_lane + ox + second) & (TILE - 1))
             chosen = jnp.where(from_lane == pick, 1.0, 0.0).astype(jnp.bfloat16)
             values = []
-            for f in range(FIELDS):
-                here = cells[f, block, pl.ds(start, CHUNKS, stride=8), :]
-                after = cells[f, block, pl.ds(start + 8, CHUNKS, stride=8), :]
+            for source, f in blocks:
+                here = source[f, pl.ds(start, CHUNKS, stride=ROWS), :]
+                after = source[f, pl.ds(start + ROWS, CHUNKS, stride=ROWS), :]
                 between = pltpu.roll(jnp.where(high_half, here, after), TILE, 1)
                 values.append(even_first * here + even_second * after + odd_weight * between)
             value = jnp.concatenate(values, axis=0)
@@ -423,18 +497,70 @@
                 preferred_element_type=jnp.float32,
             )
             mixed = (1.0 - fx) * moved[:, :LANES] + fx * moved[:, LANES:]
-            for f in range(FIELDS):
-                packed[i, k, f] = mixed[f * CHUNKS : (f + 1) * CHUNKS]
-        landing[i] = places
-
-        @pl.when(i < planes - 1)
-        def _():
-            for copy in to_plane(i):
-                copy.start()
-
+            for n, (dest, place, f) in enumerate(dests):
+                dest[place, k, f] = mixed[n * CHUNKS : (n + 1) * CHUNKS]
+
+    own_table = tuple(
+        functools.partial(lambda ref, e: ref[e], ref)
+        for ref in (donor, offset_y, offset_x, fraction_y, fraction_x)
+    )
+    for g in groups:
+
+        def find(flip, carry, g=g):
+            search(lambda e: destination[e], plane_at(behind[g], flip), (2 * g + flip) * CAP)
+            return carry
+
+        lax.fori_loop(0, 2, find, 0)
+
+    def find_near(flip, carry):
+        search(lambda e: destination[e], plane_at(0, flip), (4 + flip) * CAP)
         return carry
 
-    lax.fori_loop(0, planes // 2, fill, 0)
+    lax.fori_loop(0, 2, find_near, 0)
+    for index in range(4):
+        landing[index] = places_of(index * CAP, lambda e: receptor[e])
+    landing[4] = places_of(5 * CAP, lambda e: receptor[e])
+    landing[5] = places_of(4 * CAP, lambda e: receptor[e])
+    near_land = [land_copy(2 * g + flip, p, behind[g], flip) for g in groups for flip in range(2)]
+    near_land.append(land_copy(4, p, 0, 1))
+    for copy in near_land:
+        copy.start()
+    own_land = pltpu.make_async_copy(landing.at[5], landing_in.at[p], own_sem.at[3])
+    own_land.start()
+
+    def widths(g):
+        return range(GROUPS[g][1] - GROUPS[g][0])
+
+    for g in groups:
+
+        def fill_direct(flip, carry, g=g):
+            fill(
+                (2 * g + flip) * CAP,
+                own_table,
+                [(cells, GROUPS[g][0] + f) for f in widths(g)],
+                [(packed[g], flip, f) for f in widths(g)],
+            )
+            return carry
+
+        lax.fori_loop(0, 2, fill_direct, 0)
+
+    def fill_near(flip, carry):
+        fill(
+            (4 + flip) * CAP,
+            own_table,
+            [(cells, f) for f in range(FIELDS)],
+            [(packed[g], 7 - flip, f) for g in groups for f in widths(g)],
+        )
+        return carry
+
+    lax.fori_loop(0, 2, fill_near, 0)
+    own_tiles = [
+        pltpu.make_async_copy(packed[g].at[7], arrived[g].at[p], own_sem.at[4 + g]) for g in groups
+    ]
+    for g in groups:
+        mate_copy(g).start()
+        own_tiles[g].start()
+
     pl.semaphore_wait(beyond, 2)
 
     @pl.when(leader)
@@ -444,12 +570,6 @@
                 barrier, inc=1, device_id=(lax.rem(a + o, azims), p), device_id_type=MESH
             )
 
-    lax.fori_loop(planes // 2, planes, fill, 0)
-    own_tiles = pltpu.make_async_copy(packed.at[planes - 1], packed_in.at[p], own_sem.at[2])
-    own_land = pltpu.make_async_copy(landing.at[planes - 1], landing_in.at[p], own_sem.at[3])
-    own_tiles.start()
-    own_land.start()
-
     for copy in large[FIELDS:]:
         copy.wait()
     spread(raw_coefs, coefs)
@@ -475,6 +595,75 @@
         copy.start()
     own_tips = own_azim(tips, tips_in, tip_rows, 0)
     own_tips.start()
+
+    for g in groups:
+        raw_copy(g).wait_send()
+    for flip in range(2):
+        for g in groups:
+            direct_copy(g, flip).start()
+
+    fetches = []
+    for g in groups:
+        for copy in table_copies(g):
+            copy.wait()
+        fetches.append(pltpu.make_async_copy(integers_in.at[g], integers.at[g], table_sem.at[2 * g]))
+        fetches.append(pltpu.make_async_copy(reals_in.at[g], reals.at[g], table_sem.at[2 * g + 1]))
+    for copy in fetches:
+        copy.start()
+    for copy in fetches:
+        copy.wait()
+    for g in groups:
+
+        def find_relay(u, carry, g=g):
+            target = plane_at((1 - u // 2) * onward[g], u - 2 * (u // 2))
+            search(lambda e: integers[g, 0, e], target, (6 + 4 * g + u) * CAP)
+            return carry
+
+        lax.fori_loop(0, 4, find_relay, 0)
+    far_land = []
+    for u in range(2):
+        landing[6 + u] = places_of((6 + u) * CAP, lambda e: integers[0, 2, e])
+        far_land.append(land_copy(6 + u, plane_at(behind[0], 0), onward[0], u))
+        far_land[-1].start()
+
+    relay_own = [
+        pltpu.make_async_copy(
+            packed[g].at[4], arrived[g].at[plane_at(behind[g], 0)], own_sem.at[6 + g]
+        )
+        for g in groups
+    ]
+    for g in groups:
+        raw_copy(g).wait_recv()
+        for f in widths(g):
+            raw_cells[g][f, SPREAD:, :] = raw_cells[g][f, 0:SPREAD, :]
+        relay_table = (
+            lambda e, g=g: integers[g, 1, e],
+            lambda e, g=g: integers[g, 3, e],
+            lambda e, g=g: integers[g, 4, e],
+            lambda e, g=g: reals[g, 0, e],
+            lambda e, g=g: reals[g, 1, e],
+        )
+
+        def fill_relay(u, carry, g=g, relay_table=relay_table):
+            fill(
+                (6 + 4 * g + u) * CAP,
+                relay_table,
+                [(raw_cells[g], f) for f in widths(g)],
+                [(packed[g], 2 + u, f) for f in widths(g)],
+            )
+
+            @pl.when(u != 2)
+            def _():
+                relay_copy(g, u).start()
+
+            @pl.when(u == 2)
+            def _():
+                relay_own[g].start()
+
+            return carry
+
+        lax.fori_loop(0, 4, fill_relay, 0)
+
     own_tips.wait()
     for copy in tip_copies:
         copy.wait()
@@ -539,7 +728,7 @@
                 value = solved[r, f, at, :]
                 for i in range(4):
                     value = value - solved[r, FIELDS + i, at, :] * outside[i]
-                cells[f, r // 8, pl.ds(part * 64 + r % 8, 8, stride=8), :] = value
+                result[f, r // 8, pl.ds(part * 64 + r % 8, 8, stride=8), :] = value
         return carry
 
     lax.fori_loop(0, CHUNKS // 8, compose, 0)
@@ -548,24 +737,23 @@
         at = pl.ds(pl.multiple_of(c * LANES, LANES), LANES)
         row = pl.multiple_of(c * 8, 8)
         for f in range(FIELDS):
-            update[f, 0:8, at] = cells[f, 0, pl.ds(row, 8), :] - state[f, 0:8, at]
-            update[f, 8:12, at] = cells[f, 1, pl.ds(row, 4), :] - state[f, 8:12, at]
+            update[f, 0:8, at] = result[f, 0, pl.ds(row, 8), :] - state[f, 0:8, at]
+            update[f, 8:12, at] = result[f, 1, pl.ds(row, 4), :] - state[f, 8:12, at]
         return carry
 
     lax.fori_loop(0, CHUNKS, move, 0, unroll=4)
 
-    own_tiles.wait()
-    own_land.wait()
-
-    def settle(i, carry):
-        for copy in to_plane(i):
-            copy.wait()
-        return carry
-
-    lax.fori_loop(0, planes - 1, settle, 0)
-
-
-def finish_kernel(landing, packed, update, state, fringe, out_hbm, out, rows, cells, total, places, counts, sems):
+    for copy in [own_land] + own_tiles + relay_own + near_land + far_land:
+        copy.wait()
+    for g in groups:
+        mate_copy(g).wait()
+        for flip in range(2):
+            direct_copy(g, flip).wait()
+        for u in (3, 0, 1):
+            relay_copy(g, u).wait()
+
+
+def finish_kernel(landing, arrived0, arrived1, update, state, fringe, out_hbm, out, rows, cells, total, places, counts, sems):
     planes = landing.shape[0]
     fetch = pltpu.make_async_copy(landing, places, sems.at[FIELDS])
     fetch.start()
@@ -581,7 +769,8 @@
 
         @pl.when(row >= 0)
         def _():
-            total[row] = total[row] + packed[d, k]
+            for (low, high), source in zip(GROUPS, (arrived0, arrived1)):
+                total[row, low:high] = total[row, low:high] + source[d, k]
             counts[row] = counts[row] + 1.0
 
         return carry
@@ -646,25 +835,37 @@
     vmem = pl.BlockSpec(memory_space=pltpu.VMEM)
     hbm = pl.BlockSpec(memory_space=pltpu.HBM)
     number = pltpu.VMEM
-    packed_in, landing_in, update = pl.pallas_call(
+    wide0, wide1 = (high - low for low, high in GROUPS)
+    arrived0, arrived1, landing_in, update = pl.pallas_call(
         functools.partial(exchange_kernel, azims, planes),
         out_shape=(
-            f32(planes, CAP, FIELDS, CHUNKS, LANES),
+            f32(planes, CAP, wide0, CHUNKS, LANES),
+            f32(planes, CAP, wide1, CHUNKS, LANES),
             jax.ShapeDtypeStruct((planes, 1, LANES), jnp.int32),
             f32(FIELDS, ROWS, CELLS),
         ),
         in_specs=[hbm] * 11,
-        out_specs=(vmem,) * 3,
+        out_specs=(vmem,) * 4,
         scratch_shapes=[pltpu.SMEM((SLOTS,), jnp.int32)] * 5
         + [pltpu.SMEM((SLOTS,), jnp.float32)] * 2
         + [
-            pltpu.SMEM((planes * CAP,), jnp.int32),
+            pltpu.SMEM((14 * CAP,), jnp.int32),
+            pltpu.SMEM((2, 8, LANES), jnp.int32),
+            pltpu.SMEM((2, 8, LANES), jnp.float32),
             number((FIELDS, ROWS, CELLS), jnp.float32),
             number((3, ROWS, CELLS), jnp.float32),
-            number((FIELDS, 2, 2 * CHUNKS * 8, LANES), jnp.float32),
+            number((FIELDS, 2, CHUNKS * 8, LANES), jnp.float32),
+            number((FIELDS, 2 * SPREAD, LANES), jnp.float32),
+            number((wide0, 2 * SPREAD, LANES), jnp.float32),
+            number((wide1, 2 * SPREAD, LANES), jnp.float32),
             number((3, 2, CHUNKS * 8, LANES), jnp.float32),
-            number((planes, CAP, FIELDS, CHUNKS, LANES), jnp.float32),
-            number((planes, 1, LANES), jnp.int32),
+            number((PLACES, CAP, wide0, CHUNKS, LANES), jnp.float32),
+            number((PLACES, CAP, wide1, CHUNKS, LANES), jnp.float32),
+            number((8, 1, LANES), jnp.int32),
+            number((8, LANES), jnp.int32),
+            number((8, LANES), jnp.float32),
+            number((2, 8, LANES), jnp.int32),
+            number((2, 8, LANES), jnp.float32),
             number((ROWS, COLS, CHUNKS, LANES), jnp.float32),
             number((CHUNKS * TIPS, LANES), jnp.float32),
             number((CHUNKS * TIPS, LANES), jnp.float32),
@@ -675,15 +876,20 @@
             number((CHUNKS * BACK, LANES), jnp.float32),
             pltpu.SemaphoreType.DMA((7,)),
             pltpu.SemaphoreType.DMA((FIELDS + 3,)),
-            pltpu.SemaphoreType.DMA((planes,)),
-            pltpu.SemaphoreType.DMA((planes,)),
-            pltpu.SemaphoreType.DMA((planes,)),
-            pltpu.SemaphoreType.DMA((planes,)),
+            pltpu.SemaphoreType.DMA((2,)),
+            pltpu.SemaphoreType.DMA((2,)),
+            pltpu.SemaphoreType.DMA((4,)),
+            pltpu.SemaphoreType.DMA((4,)),
+            pltpu.SemaphoreType.DMA((4,)),
+            pltpu.SemaphoreType.DMA((2 * PLACES,)),
+            pltpu.SemaphoreType.DMA((2 * PLACES,)),
+            pltpu.SemaphoreType.DMA((8,)),
+            pltpu.SemaphoreType.DMA((8,)),
             pltpu.SemaphoreType.DMA((azims,)),
             pltpu.SemaphoreType.DMA((azims,)),
             pltpu.SemaphoreType.DMA((azims,)),
             pltpu.SemaphoreType.DMA((azims,)),
-            pltpu.SemaphoreType.DMA((4,)),
+            pltpu.SemaphoreType.DMA((8,)),
             pltpu.SemaphoreType.REGULAR,
             pltpu.SemaphoreType.REGULAR,
             pltpu.SemaphoreType.REGULAR,
@@ -713,7 +919,7 @@
     return pl.pallas_call(
         finish_kernel,
         out_shape=f32(FIELDS, ROWS, CELLS),
-        in_specs=[vmem] * 5,
+        in_specs=[vmem] * 6,
         out_specs=hbm,
         scratch_shapes=[
             number((FIELDS, ROWS, CELLS), jnp.float32),
@@ -726,7 +932,7 @@
         ],
         compiler_params=pltpu.CompilerParams(vmem_limit_bytes=32 * 2**20),
         name="finish",
-    )(landing_in, packed_in, update, state, fringe)
+    )(landing_in, arrived0, arrived1, update, state, fringe)
 
 
 def solution(mesh):

time: 39.2 us -> 39 us (level)
  the two profiles are of different devices: /device:TPU:1 before, /device:TPU:0 now
where the time goes in v4:
time: 39 us; the launch traced here: 38.9 us
  Pallas kernels  38.8 us (99%)
    pallas_call x1, Pallas kernels, local(): pl.pallas_call(functools.partial(exchange_kernel, azims, planes), out_sha...  35.8 us
    pallas_call x1, Pallas kernels, local(): pl.pallas_call(finish_kernel, out_shape=f32(FIELDS, ROWS, CELLS), in_spec...  3.04 us

profile of v4, /device:TPU:0, one launch (start us, length us, event | category | flops | bytes accessed | tf_op | source)
XLA Modules:
  0.0 38.9 jit_solution(9297938694210125466)
XLA Ops:
  0.0 0.0 copy-start
  0.0 0.0 copy-start.1
  0.0 35.8 %exchange.1 = (f32[8,4,3,32,128]{4,3,2,1,0:T(8,128)S(1)}, f32[8,4,2,32,128]{4,3,2,1,0:T(8,128)S(1)}, s32[8,1,128]{2,1,0:T(1,128)S(1)}, f32[5,12,4096]{2,1,0:T(8,128)S(1)}) custom-call(s32[16]{0:T(128)} %bitcast.1, s32[16]{0:T(128)} %donor_hbm.1, s32[16]{0:T(128)} %receptor_hbm.1, s32[16]{0:T(128)} %offset_y_hbm.1, s32[16]{0:T(128)} %offset_x_hbm.1, ...), custom_call_target="tpu_custom_call" | custom-call | tf_op jit(solution)/shard_map/exchange/pallas_call | solution.py:839
  35.8 0.0 copy-done
  35.8 0.0 copy-done.1
  35.8 3.0 %finish.1 = f32[5,12,4096]{2,1,0:T(8,128)} custom-call(s32[8,1,128]{2,1,0:T(1,128)S(1)} %get-tuple-element.9.landing, f32[8,4,3,32,128]{4,3,2,1,0:T(8,128)S(1)} %get-tuple-element.10.arrived0, f32[8,4,2,32,128]{4,3,2,1,0:T(8,128)S(1)} %get-tuple-element.11.arrived1, f32[5,12,4096]{2,1,0:T(8,128)S(1)} %get-tuple-element.12.update, ...), custom_call_target="tpu_custom_call" | custom-call | tf_op jit(solution)/shard_map/finish/pallas_call | solution.py:919
Async XLA Ops:
  0.0 35.8 %copy-start = (f32[5,12,4096]{2,1,0:T(8,128)S(1)}, f32[5,12,4096]{2,1,0:T(8,128)}, u32[]{:S(2)}) copy-start(f32[5,12,4096]{2,1,0:T(8,128)} %state.1) | copy-start | bytes 2949124
  0.0 35.8 %copy-start.1 = (s32[12,4096]{1,0:T(8,128)S(1)}, s32[12,4096]{1,0:T(8,128)}, u32[]{:S(2)}) copy-start(s32[12,4096]{1,0:T(8,128)} %fringe.1) | copy-start | bytes 589828

commit v5 on v4

--- a/solution.py
+++ b/solution.py
@@ -265,8 +265,8 @@
     back_send,
     back_recv,
     own_sem,
+    mated,
     ready,
-    beyond,
     go,
 ):
     a = lax.axis_index("azim")
@@ -313,7 +313,6 @@
 
     barrier = pltpu.get_barrier_semaphore()
     near = [(0, 1), (1, 0), (1, 1), (chips - 1, 0), (chips - 1, 1)]
-    leader = p == 0
 
     def plane_at(ahead, flip):
         return lax.rem(p // 2 + ahead, chips) * 2 + lax.rem(p + flip, 2)
@@ -332,11 +331,12 @@
     behind = (onward[1], onward[0])
 
     for ahead, flip in near:
-        there = plane_at(ahead, flip)
-
-        @pl.when(there != 0)
+
+        @pl.when(lax.rem(core + flip, 2) == 1)
         def _():
-            pl.semaphore_signal(barrier, inc=1, device_id=(a, there), device_id_type=MESH)
+            pl.semaphore_signal(
+                barrier, inc=1, device_id=(a, plane_at(ahead, flip)), device_id_type=MESH
+            )
 
     def to_azim(source, dest, rows, send, recv, o):
         there = lax.rem(a + o, azims)
@@ -418,25 +418,36 @@
         large[f].wait()
         spread_twice(state.at[f], cells.at[f])
 
-    @pl.when(jnp.logical_not(leader))
+    @pl.when(core == 1)
     def _():
         pl.semaphore_wait(barrier, len(near))
-
-    @pl.when(jnp.logical_not(leader) & (p // 2 != chips // 2))
+        pl.semaphore_signal(mated, inc=1, device_id=(a, plane_at(0, 1)), device_id_type=MESH)
+        for ahead in (1, chips - 1):
+            pl.semaphore_signal(ready, inc=1, device_id=(a, plane_at(ahead, 1)), device_id_type=MESH)
+
+    @pl.when(core == 0)
     def _():
-        pl.semaphore_signal(ready, inc=1, device_id=(a, 0), device_id_type=MESH)
-
-    @pl.when(leader)
-    def _():
-        pl.semaphore_wait(ready, len(near))
+        pl.semaphore_wait(mated, 1)
+        for o in range(1, azims):
+            pl.semaphore_signal(
+                barrier, inc=1, device_id=(lax.rem(a + o, azims), p), device_id_type=MESH
+            )
+        pl.semaphore_wait(ready, 2)
 
     for g in groups:
         for copy in table_copies(g):
             copy.start()
     for g in groups:
         raw_copy(g).start()
-    for ahead in (1, chips - 1):
-        pl.semaphore_signal(beyond, inc=1, device_id=(a, plane_at(ahead, 0)), device_id_type=MESH)
+    for copy in large[FIELDS:]:
+        copy.wait()
+    spread(raw_coefs, coefs)
+
+    def one_part(part, carry):
+        eliminate(cells, coefs, solved, tips, part)
+        return carry
+
+    lax.fori_loop(0, CHUNKS // 8, one_part, 0)
 
     def search(named, target, base):
         seen = jnp.int32(0)
@@ -561,32 +572,12 @@
         mate_copy(g).start()
         own_tiles[g].start()
 
-    pl.semaphore_wait(beyond, 2)
-
-    @pl.when(leader)
-    def _():
-        for o in range(1, azims):
-            pl.semaphore_signal(
-                barrier, inc=1, device_id=(lax.rem(a + o, azims), p), device_id_type=MESH
-            )
-
-    for copy in large[FIELDS:]:
-        copy.wait()
-    spread(raw_coefs, coefs)
-
-    def one_part(part, carry):
-        eliminate(cells, coefs, solved, tips, part)
-        return carry
-
-    lax.fori_loop(0, CHUNKS // 8, one_part, 0)
-
-    @pl.when(leader)
+    @pl.when(core == 0)
     def _():
         pl.semaphore_wait(barrier, azims - 1)
-        for o in range(1, planes):
-            pl.semaphore_signal(go, inc=1, device_id=(a, o), device_id_type=MESH)
-
-    @pl.when(jnp.logical_not(leader))
+        pl.semaphore_signal(go, inc=1, device_id=(a, plane_at(0, 1)), device_id_type=MESH)
+
+    @pl.when(core == 1)
     def _():
         pl.semaphore_wait(go, 1)
 

time: 39 us -> 36.3 us (0.931)
  the two profiles are of different devices: /device:TPU:0 before, /device:TPU:1 now
where the time goes in v5:
time: 36.3 us; the launch traced here: 35.9 us
  Pallas kernels  35.8 us (99%)
    pallas_call x1, Pallas kernels, local(): pl.pallas_call(functools.partial(exchange_kernel, azims, planes), out_sha...  32.8 us
    pallas_call x1, Pallas kernels, local(): pl.pallas_call(finish_kernel, out_shape=f32(FIELDS, ROWS, CELLS), in_spec...  3.04 us

profile of v5, /device:TPU:1, one launch (start us, length us, event | category | flops | bytes accessed | tf_op | source)
XLA Modules:
  0.0 35.9 jit_solution(4946406843692872968)
XLA Ops:
  0.0 0.0 copy-start
  0.0 0.0 copy-start.1
  0.0 32.8 %exchange.1 = (f32[8,4,3,32,128]{4,3,2,1,0:T(8,128)S(1)}, f32[8,4,2,32,128]{4,3,2,1,0:T(8,128)S(1)}, s32[8,1,128]{2,1,0:T(1,128)S(1)}, f32[5,12,4096]{2,1,0:T(8,128)S(1)}) custom-call(s32[16]{0:T(128)} %bitcast.1, s32[16]{0:T(128)} %donor_hbm.1, s32[16]{0:T(128)} %receptor_hbm.1, s32[16]{0:T(128)} %offset_y_hbm.1, s32[16]{0:T(128)} %offset_x_hbm.1, ...), custom_call_target="tpu_custom_call" | custom-call | tf_op jit(solution)/shard_map/exchange/pallas_call | solution.py:830
  32.8 0.0 copy-done
  32.8 0.0 copy-done.1
  32.8 3.0 %finish.1 = f32[5,12,4096]{2,1,0:T(8,128)} custom-call(s32[8,1,128]{2,1,0:T(1,128)S(1)} %get-tuple-element.9.landing, f32[8,4,3,32,128]{4,3,2,1,0:T(8,128)S(1)} %get-tuple-element.10.arrived0, f32[8,4,2,32,128]{4,3,2,1,0:T(8,128)S(1)} %get-tuple-element.11.arrived1, f32[5,12,4096]{2,1,0:T(8,128)S(1)} %get-tuple-element.12.update, ...), custom_call_target="tpu_custom_call" | custom-call | tf_op jit(solution)/shard_map/finish/pallas_call | solution.py:910
Async XLA Ops:
  0.0 32.8 %copy-start = (f32[5,12,4096]{2,1,0:T(8,128)S(1)}, f32[5,12,4096]{2,1,0:T(8,128)}, u32[]{:S(2)}) copy-start(f32[5,12,4096]{2,1,0:T(8,128)} %state.1) | copy-start | bytes 2949124
  0.0 32.8 %copy-start.1 = (s32[12,4096]{1,0:T(8,128)S(1)}, s32[12,4096]{1,0:T(8,128)}, u32[]{:S(2)}) copy-start(s32[12,4096]{1,0:T(8,128)} %fringe.1) | copy-start | bytes 589828

commit v6 on v5

--- a/solution.py
+++ b/solution.py
@@ -338,6 +338,15 @@
                 barrier, inc=1, device_id=(a, plane_at(ahead, flip)), device_id_type=MESH
             )
 
+    for o in range(1, azims):
+        pl.semaphore_signal(
+            barrier, inc=1, device_id=(lax.rem(a + o, azims), p - core), device_id_type=MESH
+        )
+
+    @pl.when(core == 1)
+    def _():
+        pl.semaphore_signal(barrier, inc=1, device_id=(a, plane_at(0, 1)), device_id_type=MESH)
+
     def to_azim(source, dest, rows, send, recv, o):
         there = lax.rem(a + o, azims)
         return pltpu.make_async_remote_copy(
@@ -428,10 +437,6 @@
     @pl.when(core == 0)
     def _():
         pl.semaphore_wait(mated, 1)
-        for o in range(1, azims):
-            pl.semaphore_signal(
-                barrier, inc=1, device_id=(lax.rem(a + o, azims), p), device_id_type=MESH
-            )
         pl.semaphore_wait(ready, 2)
 
     for g in groups:
@@ -555,6 +560,21 @@
 
         lax.fori_loop(0, 2, fill_direct, 0)
 
+    @pl.when(core == 0)
+    def _():
+        pl.semaphore_wait(barrier, 2 * azims - 1)
+        pl.semaphore_signal(go, inc=1, device_id=(a, plane_at(0, 1)), device_id_type=MESH)
+
+    @pl.when(core == 1)
+    def _():
+        pl.semaphore_wait(go, 1)
+
+    tip_copies = [to_azim(tips, tips_in, tip_rows, tips_send, tips_recv, o) for o in range(1, azims)]
+    for copy in tip_copies:
+        copy.start()
+    own_tips = own_azim(tips, tips_in, tip_rows, 0)
+    own_tips.start()
+
     def fill_near(flip, carry):
         fill(
             (4 + flip) * CAP,
@@ -571,21 +591,6 @@
     for g in groups:
         mate_copy(g).start()
         own_tiles[g].start()
-
-    @pl.when(core == 0)
-    def _():
-        pl.semaphore_wait(barrier, azims - 1)
-        pl.semaphore_signal(go, inc=1, device_id=(a, plane_at(0, 1)), device_id_type=MESH)
-
-    @pl.when(core == 1)
-    def _():
-        pl.semaphore_wait(go, 1)
-
-    tip_copies = [to_azim(tips, tips_in, tip_rows, tips_send, tips_recv, o) for o in range(1, azims)]
-    for copy in tip_copies:
-        copy.start()
-    own_tips = own_azim(tips, tips_in, tip_rows, 0)
-    own_tips.start()
 
     for g in groups:
         raw_copy(g).wait_send()
@@ -623,37 +628,31 @@
         )
         for g in groups
     ]
+    def fill_relay(g, u):
+        fill(
+            (6 + 4 * g + u) * CAP,
+            (
+                lambda e: integers[g, 1, e],
+                lambda e: integers[g, 3, e],
+                lambda e: integers[g, 4, e],
+                lambda e: reals[g, 0, e],
+                lambda e: reals[g, 1, e],
+            ),
+            [(raw_cells[g], f) for f in widths(g)],
+            [(packed[g], 2 + u, f) for f in widths(g)],
+        )
+
     for g in groups:
         raw_copy(g).wait_recv()
         for f in widths(g):
             raw_cells[g][f, SPREAD:, :] = raw_cells[g][f, 0:SPREAD, :]
-        relay_table = (
-            lambda e, g=g: integers[g, 1, e],
-            lambda e, g=g: integers[g, 3, e],
-            lambda e, g=g: integers[g, 4, e],
-            lambda e, g=g: reals[g, 0, e],
-            lambda e, g=g: reals[g, 1, e],
-        )
-
-        def fill_relay(u, carry, g=g, relay_table=relay_table):
-            fill(
-                (6 + 4 * g + u) * CAP,
-                relay_table,
-                [(raw_cells[g], f) for f in widths(g)],
-                [(packed[g], 2 + u, f) for f in widths(g)],
-            )
-
-            @pl.when(u != 2)
-            def _():
-                relay_copy(g, u).start()
-
-            @pl.when(u == 2)
-            def _():
-                relay_own[g].start()
-
+
+        def fill_onward(u, carry, g=g):
+            fill_relay(g, u)
+            relay_copy(g, u).start()
             return carry
 
-        lax.fori_loop(0, 4, fill_relay, 0)
+        lax.fori_loop(0, 2, fill_onward, 0)
 
     own_tips.wait()
     for copy in tip_copies:
@@ -703,6 +702,16 @@
         copy.start()
     own_back = own_azim(answers, borders, back_rows, 1)
     own_back.start()
+    for g in groups:
+
+        def fill_chip(u, carry, g=g):
+            fill_relay(g, u)
+            return carry
+
+        lax.fori_loop(2, 4, fill_chip, 0)
+        relay_own[g].start()
+        relay_copy(g, 3).start()
+
     own_back.wait()
     for copy in back_copies:
         copy.wait()
@@ -748,7 +757,7 @@
     planes = landing.shape[0]
     fetch = pltpu.make_async_copy(landing, places, sems.at[FIELDS])
     fetch.start()
-    for r in range(ROWS):
+    for r in range(ROWS + 1):
         counts[r] = 0.0
     total[...] = jnp.zeros(total.shape, jnp.float32)
     fetch.wait()
@@ -758,15 +767,13 @@
         k = slot - d * CAP
         row = places[d, 0, k]
 
-        @pl.when(row >= 0)
-        def _():
-            for (low, high), source in zip(GROUPS, (arrived0, arrived1)):
-                total[row, low:high] = total[row, low:high] + source[d, k]
-            counts[row] = counts[row] + 1.0
-
+        row = jnp.where(row >= 0, row, ROWS)
+        for (low, high), source in zip(GROUPS, (arrived0, arrived1)):
+            total[row, low:high] = total[row, low:high] + source[d, k]
+        counts[row] = counts[row] + 1.0
         return carry
 
-    lax.fori_loop(0, planes * CAP, add, 0)
+    lax.fori_loop(0, planes * CAP, add, 0, unroll=4)
 
     for b in range(2):
         line = lax.broadcasted_iota(jnp.int32, (8, LANES), 0) + 8 * b
@@ -916,9 +923,9 @@
             number((FIELDS, ROWS, CELLS), jnp.float32),
             number((4, 8, LANES), jnp.float32),
             number((2, CHUNKS * 8, LANES), jnp.float32),
-            number((ROWS, FIELDS, CHUNKS, LANES), jnp.float32),
+            number((ROWS + 1, FIELDS, CHUNKS, LANES), jnp.float32),
             pltpu.SMEM((planes, 1, LANES), jnp.int32),
-            pltpu.SMEM((ROWS,), jnp.float32),
+            pltpu.SMEM((ROWS + 1,), jnp.float32),
             pltpu.SemaphoreType.DMA((FIELDS + 1,)),
         ],
         compiler_params=pltpu.CompilerParams(vmem_limit_bytes=32 * 2**20),

time: 36.3 us -> 34.9 us (0.961)
  Pallas kernels: 35.8 us -> 34.7 us
    pallas_call x1, Pallas kernels: 32.8 us -> 32.1 us  [local(): pl.pallas_call(functools.partial(exchange_kernel, azims, planes), out_sha...]
    pallas_call x1, Pallas kernels: 3.04 us -> 2.65 us  [local(): pl.pallas_call(finish_kernel, out_shape=f32(FIELDS, ROWS, CELLS), in_spec...]
where the time goes in v6:
time: 34.9 us; the launch traced here: 34.8 us
  Pallas kernels  34.7 us (99%)
    pallas_call x1, Pallas kernels, local(): pl.pallas_call(functools.partial(exchange_kernel, azims, planes), out_sha...  32.1 us
    pallas_call x1, Pallas kernels, local(): pl.pallas_call(finish_kernel, out_shape=f32(FIELDS, ROWS, CELLS), in_spec...  2.65 us

profile of v6, /device:TPU:1, one launch (start us, length us, event | category | flops | bytes accessed | tf_op | source)
XLA Modules:
  0.0 34.8 jit_solution(3127153091258071577)
XLA Ops:
  0.0 0.0 copy-start
  0.0 0.0 copy-start.1
  0.0 32.1 %exchange.1 = (f32[8,4,3,32,128]{4,3,2,1,0:T(8,128)S(1)}, f32[8,4,2,32,128]{4,3,2,1,0:T(8,128)S(1)}, s32[8,1,128]{2,1,0:T(1,128)S(1)}, f32[5,12,4096]{2,1,0:T(8,128)S(1)}) custom-call(s32[16]{0:T(128)} %bitcast.1, s32[16]{0:T(128)} %donor_hbm.1, s32[16]{0:T(128)} %receptor_hbm.1, s32[16]{0:T(128)} %offset_y_hbm.1, s32[16]{0:T(128)} %offset_x_hbm.1, ...), custom_call_target="tpu_custom_call" | custom-call | tf_op jit(solution)/shard_map/exchange/pallas_call | solution.py:837
  32.1 0.0 copy-done
  32.1 0.0 copy-done.1
  32.1 2.7 %finish.1 = f32[5,12,4096]{2,1,0:T(8,128)} custom-call(s32[8,1,128]{2,1,0:T(1,128)S(1)} %get-tuple-element.9.landing, f32[8,4,3,32,128]{4,3,2,1,0:T(8,128)S(1)} %get-tuple-element.10.arrived0, f32[8,4,2,32,128]{4,3,2,1,0:T(8,128)S(1)} %get-tuple-element.11.arrived1, f32[5,12,4096]{2,1,0:T(8,128)S(1)} %get-tuple-element.12.update, ...), custom_call_target="tpu_custom_call" | custom-call | tf_op jit(solution)/shard_map/finish/pallas_call | solution.py:917
Async XLA Ops:
  0.0 32.1 %copy-start = (f32[5,12,4096]{2,1,0:T(8,128)S(1)}, f32[5,12,4096]{2,1,0:T(8,128)}, u32[]{:S(2)}) copy-start(f32[5,12,4096]{2,1,0:T(8,128)} %state.1) | copy-start | bytes 2949124
  0.0 32.1 %copy-start.1 = (s32[12,4096]{1,0:T(8,128)S(1)}, s32[12,4096]{1,0:T(8,128)}, u32[]{:S(2)}) copy-start(s32[12,4096]{1,0:T(8,128)} %fringe.1) | copy-start | bytes 589828

commit v7 on v6

--- a/solution.py
+++ b/solution.py
@@ -21,6 +21,7 @@
 MESH = pl.DeviceIdType.MESH
 GROUPS = ((0, 3), (3, FIELDS))
 PLACES = 8
+ORDER = (0, 3, 1, 4, 2)
 SPREAD = CHUNKS * ROWS
 TIP_ROW = {0: 0, 1: 1, ROWS - 2: 2, ROWS - 1: 3}
 
@@ -362,13 +363,13 @@
         at = pl.ds(pl.multiple_of(a * rows, 8), rows)
         return pltpu.make_async_copy(source.at[at, :], dest.at[at, :], own_sem.at[index])
 
-    def raw_copy(g):
-        low, high = GROUPS[g]
+    def raw_copy(f):
+        g = 0 if f < GROUPS[0][1] else 1
         return remote(
-            cells.at[low:high, 0:SPREAD, :],
-            raw_cells[g].at[:, 0:SPREAD, :],
-            raw_send.at[g],
-            raw_recv.at[g],
+            cells.at[f, 0:SPREAD, :],
+            raw_cells[g].at[f - GROUPS[g][0], 0:SPREAD, :],
+            raw_send.at[f],
+            raw_recv.at[f],
             plane_at(onward[g], 0),
         )
 
@@ -423,9 +424,10 @@
             value = jnp.where(spot == e, source[e], value)
         reals_out[line : line + 1, :] = value
 
-    for f in range(FIELDS):
-        large[f].wait()
-        spread_twice(state.at[f], cells.at[f])
+    def send_tables():
+        for g in groups:
+            for copy in table_copies(g):
+                copy.start()
 
     @pl.when(core == 1)
     def _():
@@ -433,17 +435,24 @@
         pl.semaphore_signal(mated, inc=1, device_id=(a, plane_at(0, 1)), device_id_type=MESH)
         for ahead in (1, chips - 1):
             pl.semaphore_signal(ready, inc=1, device_id=(a, plane_at(ahead, 1)), device_id_type=MESH)
+        send_tables()
+
+    for f in ORDER:
+        large[f].wait()
+        spread_twice(state.at[f], cells.at[f])
+
+        @pl.when(core == 1)
+        def _():
+            raw_copy(f).start()
 
     @pl.when(core == 0)
     def _():
         pl.semaphore_wait(mated, 1)
         pl.semaphore_wait(ready, 2)
-
-    for g in groups:
-        for copy in table_copies(g):
-            copy.start()
-    for g in groups:
-        raw_copy(g).start()
+        send_tables()
+        for f in ORDER:
+            raw_copy(f).start()
+
     for copy in large[FIELDS:]:
         copy.wait()
     spread(raw_coefs, coefs)
@@ -592,8 +601,8 @@
         mate_copy(g).start()
         own_tiles[g].start()
 
-    for g in groups:
-        raw_copy(g).wait_send()
+    for f in ORDER:
+        raw_copy(f).wait_send()
     for flip in range(2):
         for g in groups:
             direct_copy(g, flip).start()
@@ -643,8 +652,8 @@
         )
 
     for g in groups:
-        raw_copy(g).wait_recv()
         for f in widths(g):
+            raw_copy(GROUPS[g][0] + f).wait_recv()
             raw_cells[g][f, SPREAD:, :] = raw_cells[g][f, 0:SPREAD, :]
 
         def fill_onward(u, carry, g=g):
@@ -874,8 +883,8 @@
             number((CHUNKS * BACK, LANES), jnp.float32),
             pltpu.SemaphoreType.DMA((7,)),
             pltpu.SemaphoreType.DMA((FIELDS + 3,)),
-            pltpu.SemaphoreType.DMA((2,)),
-            pltpu.SemaphoreType.DMA((2,)),
+            pltpu.SemaphoreType.DMA((FIELDS,)),
+            pltpu.SemaphoreType.DMA((FIELDS,)),
             pltpu.SemaphoreType.DMA((4,)),
             pltpu.SemaphoreType.DMA((4,)),
             pltpu.SemaphoreType.DMA((4,)),

time: 34.9 us -> 34.6 us (level)
  no operation moved by 1% of the time
where the time goes in v7:
time: 34.6 us; the launch traced here: 34.5 us
  Pallas kernels  34.4 us (99%)
    pallas_call x1, Pallas kernels, local(): pl.pallas_call(functools.partial(exchange_kernel, azims, planes), out_sha...  31.8 us
    pallas_call x1, Pallas kernels, local(): pl.pallas_call(finish_kernel, out_shape=f32(FIELDS, ROWS, CELLS), in_spec...  2.65 us

profile of v7, /device:TPU:1, one launch (start us, length us, event | category | flops | bytes accessed | tf_op | source)
XLA Modules:
  0.0 34.5 jit_solution(8940127447848339163)
XLA Ops:
  0.0 0.0 copy-start
  0.0 0.0 copy-start.1
  0.0 31.8 %exchange.1 = (f32[8,4,3,32,128]{4,3,2,1,0:T(8,128)S(1)}, f32[8,4,2,32,128]{4,3,2,1,0:T(8,128)S(1)}, s32[8,1,128]{2,1,0:T(1,128)S(1)}, f32[5,12,4096]{2,1,0:T(8,128)S(1)}) custom-call(s32[16]{0:T(128)} %bitcast.1, s32[16]{0:T(128)} %donor_hbm.1, s32[16]{0:T(128)} %receptor_hbm.1, s32[16]{0:T(128)} %offset_y_hbm.1, s32[16]{0:T(128)} %offset_x_hbm.1, ...), custom_call_target="tpu_custom_call" | custom-call | tf_op jit(solution)/shard_map/exchange/pallas_call | solution.py:846
  31.8 0.0 copy-done
  31.8 0.0 copy-done.1
  31.8 2.7 %finish.1 = f32[5,12,4096]{2,1,0:T(8,128)} custom-call(s32[8,1,128]{2,1,0:T(1,128)S(1)} %get-tuple-element.9.landing, f32[8,4,3,32,128]{4,3,2,1,0:T(8,128)S(1)} %get-tuple-element.10.arrived0, f32[8,4,2,32,128]{4,3,2,1,0:T(8,128)S(1)} %get-tuple-element.11.arrived1, f32[5,12,4096]{2,1,0:T(8,128)S(1)} %get-tuple-element.12.update, ...), custom_call_target="tpu_custom_call" | custom-call | tf_op jit(solution)/shard_map/finish/pallas_call | solution.py:926
Async XLA Ops:
  0.0 31.8 %copy-start = (f32[5,12,4096]{2,1,0:T(8,128)S(1)}, f32[5,12,4096]{2,1,0:T(8,128)}, u32[]{:S(2)}) copy-start(f32[5,12,4096]{2,1,0:T(8,128)} %state.1) | copy-start | bytes 2949124
  0.0 31.8 %copy-start.1 = (s32[12,4096]{1,0:T(8,128)S(1)}, s32[12,4096]{1,0:T(8,128)}, u32[]{:S(2)}) copy-start(s32[12,4096]{1,0:T(8,128)} %fringe.1) | copy-start | bytes 589828

commit v8 on v7

--- a/solution.py
+++ b/solution.py
@@ -601,11 +601,12 @@
         mate_copy(g).start()
         own_tiles[g].start()
 
-    for f in ORDER:
+    for f in ORDER[:4]:
         raw_copy(f).wait_send()
     for flip in range(2):
         for g in groups:
             direct_copy(g, flip).start()
+    raw_copy(ORDER[4]).wait_send()
 
     fetches = []
     for g in groups:
@@ -651,17 +652,20 @@
             [(packed[g], 2 + u, f) for f in widths(g)],
         )
 
-    for g in groups:
-        for f in widths(g):
-            raw_copy(GROUPS[g][0] + f).wait_recv()
-            raw_cells[g][f, SPREAD:, :] = raw_cells[g][f, 0:SPREAD, :]
-
-        def fill_onward(u, carry, g=g):
-            fill_relay(g, u)
-            relay_copy(g, u).start()
-            return carry
-
-        lax.fori_loop(0, 2, fill_onward, 0)
+    def pass_on():
+        for g in groups:
+            for f in widths(g):
+                raw_copy(GROUPS[g][0] + f).wait_recv()
+                raw_cells[g][f, SPREAD:, :] = raw_cells[g][f, 0:SPREAD, :]
+
+            def fill_onward(u, carry, g=g):
+                fill_relay(g, u)
+                relay_copy(g, u).start()
+                return carry
+
+            lax.fori_loop(0, 2, fill_onward, 0)
+
+    pl.when(core == 1)(pass_on)
 
     own_tips.wait()
     for copy in tip_copies:
@@ -711,6 +715,8 @@
         copy.start()
     own_back = own_azim(answers, borders, back_rows, 1)
     own_back.start()
+    pl.when(core == 0)(pass_on)
+
     for g in groups:
 
         def fill_chip(u, carry, g=g):

time: 34.6 us -> 34.6 us (level)
  no operation moved by 1% of the time
where the time goes in v8:
time: 34.6 us; the launch traced here: 34.5 us
  Pallas kernels  34.4 us (99%)
    pallas_call x1, Pallas kernels, local(): pl.pallas_call(functools.partial(exchange_kernel, azims, planes), out_sha...  31.8 us
    pallas_call x1, Pallas kernels, local(): pl.pallas_call(finish_kernel, out_shape=f32(FIELDS, ROWS, CELLS), in_spec...  2.65 us

profile of v8, /device:TPU:1, one launch (start us, length us, event | category | flops | bytes accessed | tf_op | source)
XLA Modules:
  0.0 34.5 jit_solution(4226141996595570915)
XLA Ops:
  0.0 0.0 copy-start
  0.0 0.0 copy-start.1
  0.0 31.8 %exchange.1 = (f32[8,4,3,32,128]{4,3,2,1,0:T(8,128)S(1)}, f32[8,4,2,32,128]{4,3,2,1,0:T(8,128)S(1)}, s32[8,1,128]{2,1,0:T(1,128)S(1)}, f32[5,12,4096]{2,1,0:T(8,128)S(1)}) custom-call(s32[16]{0:T(128)} %bitcast.1, s32[16]{0:T(128)} %donor_hbm.1, s32[16]{0:T(128)} %receptor_hbm.1, s32[16]{0:T(128)} %offset_y_hbm.1, s32[16]{0:T(128)} %offset_x_hbm.1, ...), custom_call_target="tpu_custom_call" | custom-call | tf_op jit(solution)/shard_map/exchange/pallas_call | solution.py:852
  31.8 0.0 copy-done
  31.8 0.0 copy-done.1
  31.8 2.7 %finish.1 = f32[5,12,4096]{2,1,0:T(8,128)} custom-call(s32[8,1,128]{2,1,0:T(1,128)S(1)} %get-tuple-element.9.landing, f32[8,4,3,32,128]{4,3,2,1,0:T(8,128)S(1)} %get-tuple-element.10.arrived0, f32[8,4,2,32,128]{4,3,2,1,0:T(8,128)S(1)} %get-tuple-element.11.arrived1, f32[5,12,4096]{2,1,0:T(8,128)S(1)} %get-tuple-element.12.update, ...), custom_call_target="tpu_custom_call" | custom-call | tf_op jit(solution)/shard_map/finish/pallas_call | solution.py:932
Async XLA Ops:
  0.0 31.8 %copy-start = (f32[5,12,4096]{2,1,0:T(8,128)S(1)}, f32[5,12,4096]{2,1,0:T(8,128)}, u32[]{:S(2)}) copy-start(f32[5,12,4096]{2,1,0:T(8,128)} %state.1) | copy-start | bytes 2949124
  0.0 31.8 %copy-start.1 = (s32[12,4096]{1,0:T(8,128)S(1)}, s32[12,4096]{1,0:T(8,128)}, u32[]{:S(2)}) copy-start(s32[12,4096]{1,0:T(8,128)} %fringe.1) | copy-start | bytes 589828

commit v9 on v8

--- a/solution.py
+++ b/solution.py
@@ -788,7 +788,7 @@
         counts[row] = counts[row] + 1.0
         return carry
 
-    lax.fori_loop(0, planes * CAP, add, 0, unroll=4)
+    lax.fori_loop(0, planes * CAP, add, 0, unroll=8)
 
     for b in range(2):
         line = lax.broadcasted_iota(jnp.int32, (8, LANES), 0) + 8 * b
@@ -817,7 +817,7 @@
                 )
             return carry
 
-        lax.fori_loop(0, CHUNKS, move, 0, unroll=4)
+        lax.fori_loop(0, CHUNKS, move, 0, unroll=8)
         copy = pltpu.make_async_copy(out.at[f], out_hbm.at[f], sems.at[f])
         copy.start()
         copies.append(copy)

time: 34.6 us -> 34.4 us (level)
  no operation moved by 1% of the time
where the time goes in v9:
time: 34.4 us; the launch traced here: 34.3 us
  Pallas kernels  34.3 us (100%)
    pallas_call x1, Pallas kernels, local(): pl.pallas_call(functools.partial(exchange_kernel, azims, planes), out_sha...  31.8 us
    pallas_call x1, Pallas kernels, local(): pl.pallas_call(finish_kernel, out_shape=f32(FIELDS, ROWS, CELLS), in_spec...  2.54 us

profile of v9, /device:TPU:1, one launch (start us, length us, event | category | flops | bytes accessed | tf_op | source)
XLA Modules:
  0.0 34.3 jit_solution(5924950462771749012)
XLA Ops:
  0.0 0.0 copy-start
  0.0 0.0 copy-start.1
  0.0 31.8 %exchange.1 = (f32[8,4,3,32,128]{4,3,2,1,0:T(8,128)S(1)}, f32[8,4,2,32,128]{4,3,2,1,0:T(8,128)S(1)}, s32[8,1,128]{2,1,0:T(1,128)S(1)}, f32[5,12,4096]{2,1,0:T(8,128)S(1)}) custom-call(s32[16]{0:T(128)} %bitcast.1, s32[16]{0:T(128)} %donor_hbm.1, s32[16]{0:T(128)} %receptor_hbm.1, s32[16]{0:T(128)} %offset_y_hbm.1, s32[16]{0:T(128)} %offset_x_hbm.1, ...), custom_call_target="tpu_custom_call" | custom-call | tf_op jit(solution)/shard_map/exchange/pallas_call | solution.py:852
  31.8 0.0 copy-done
  31.8 0.0 copy-done.1
  31.8 2.5 %finish.1 = f32[5,12,4096]{2,1,0:T(8,128)} custom-call(s32[8,1,128]{2,1,0:T(1,128)S(1)} %get-tuple-element.9.landing, f32[8,4,3,32,128]{4,3,2,1,0:T(8,128)S(1)} %get-tuple-element.10.arrived0, f32[8,4,2,32,128]{4,3,2,1,0:T(8,128)S(1)} %get-tuple-element.11.arrived1, f32[5,12,4096]{2,1,0:T(8,128)S(1)} %get-tuple-element.12.update, ...), custom_call_target="tpu_custom_call" | custom-call | tf_op jit(solution)/shard_map/finish/pallas_call | solution.py:932
Async XLA Ops:
  0.0 31.8 %copy-start = (f32[5,12,4096]{2,1,0:T(8,128)S(1)}, f32[5,12,4096]{2,1,0:T(8,128)}, u32[]{:S(2)}) copy-start(f32[5,12,4096]{2,1,0:T(8,128)} %state.1) | copy-start | bytes 2949124
  0.0 31.8 %copy-start.1 = (s32[12,4096]{1,0:T(8,128)S(1)}, s32[12,4096]{1,0:T(8,128)}, u32[]{:S(2)}) copy-start(s32[12,4096]{1,0:T(8,128)} %fringe.1) | copy-start | bytes 589828
